TPU v7x, 128 devices: a whole 4x4x4 slice. The times are simulated.
128 devices in a mesh: grp: 16 (over x, y), dev: 8 (over z, core).
Axes of the slice: x: 4, y: 4, z: 4, core: 2. Of those that a mesh axis runs over, the one named last changes fastest.
Arguments:
- queries: bfloat16 [16384, 4096], P(('grp', 'dev')), may hold values from -2 to 2
- passages: bfloat16 [16384, 4096], P(('grp', 'dev')), may hold values from -2 to 2
- destination: int32 [16384, 1], P(('grp', 'dev')), may hold values from 0 to 127; in each aligned block of 128 rows (0 to 127, 128 to 255, ...) at most 2 rows name the same one
Outputs:
- query_grads: bfloat16 [16384, 4096], P(('grp', 'dev'))
- passage_grads: bfloat16 [16384, 4096], P(('grp', 'dev'))
Inputs may be any that keep to these rules, and one draw needn't show every extreme that they name: The pairs of one device send at most 2 pairs to one destination device, and exactly 2 in some device.
All inputs are finite; a program needn't handle non-finite values.
Results may differ from a plain program's by a relative error of at most 0.008.
Values may be sent and summed in bfloat16 or wider, within the bound.
A program may use at most 128 MiB of HBM per device.

v0:
```python
import jax
import jax.numpy as jnp
from jax import lax
from jax.sharding import PartitionSpec as P

inverse_temp = 100.0


def route_out(payload, filled_flags):
    return (
        lax.all_to_all(payload, ("grp", "dev"), split_axis=0, concat_axis=0, tiled=True),
        lax.all_to_all(filled_flags, ("grp", "dev"), split_axis=0, concat_axis=0, tiled=True),
    )


def route_back(gradient_rows):
    return lax.all_to_all(gradient_rows, ("grp", "dev"), split_axis=0, concat_axis=0, tiled=True)


def local(queries, passages, destination):
    n_group = lax.axis_size("grp")
    n_member = lax.axis_size("dev")
    n_all = n_group * n_member
    npairs = queries.shape[0]
    width_d = queries.shape[1]
    capacity = max(2, 2 * npairs // n_all)
    slots = n_all * capacity
    target = destination[:, 0]
    row_order = jnp.arange(npairs)
    earlier = row_order[None, :] < row_order[:, None]
    rank_index = jnp.sum(((target[:, None] == target[None, :]) & earlier).astype(jnp.int32), axis=1)
    slot_index = target * capacity + rank_index
    placer = (jnp.arange(slots)[:, None] == slot_index[None, :]).astype(jnp.bfloat16)
    stacked = jnp.concatenate([queries, passages], axis=1)
    payload = jnp.dot(placer, stacked, preferred_element_type=jnp.float32).astype(jnp.bfloat16)
    filled_flags = jnp.sum(placer.astype(jnp.float32), axis=1).astype(jnp.bfloat16)
    received_rows, slot_marks = route_out(
        payload.reshape(n_all, capacity, 2 * width_d), filled_flags.reshape(n_all, capacity)
    )
    received_rows = received_rows.reshape(slots, 2 * width_d)
    slot_marks = slot_marks.reshape(slots)
    query_valid = slot_marks.astype(jnp.float32)
    q_here = received_rows[:, :width_d]
    p_here = received_rows[:, width_d:]
    p_all, v_all = (
        lax.all_gather(p_here, "dev", axis=0, tiled=True),
        lax.all_gather(slot_marks, "dev", axis=0, tiled=True),
    )
    scores = inverse_temp * lax.dot_general(
        q_here, p_all, (((1,), (1,)), ((), ())), preferred_element_type=jnp.float32
    )
    scores = jnp.where(v_all.astype(jnp.float32)[None, :] > 0, scores, -1e30)
    row_max = jnp.max(scores, axis=1, keepdims=True)
    exp_scores = jnp.exp(scores - row_max)
    softmax_bf = (
        exp_scores / jnp.sum(exp_scores, axis=1, keepdims=True) * query_valid[:, None]
    ).astype(jnp.bfloat16)
    query_grad = (
        inverse_temp
        * (
            jnp.dot(softmax_bf, p_all, preferred_element_type=jnp.float32)
            - query_valid[:, None] * p_here.astype(jnp.float32)
        )
    ).astype(jnp.bfloat16)
    first_row = lax.axis_index("dev") * slots
    block_term = lax.dot_general(
        softmax_bf, q_here, (((0,), (0,)), ((), ())), preferred_element_type=jnp.float32
    )
    local_row = jnp.arange(slots * lax.axis_size("dev")) - first_row
    inside = ((local_row >= 0) & (local_row < slots)).astype(jnp.float32)
    local_index = jnp.clip(local_row, 0, slots - 1)
    own_rows = jnp.take(q_here, local_index, axis=0).astype(jnp.float32)
    own_rows = own_rows * (inside * jnp.take(query_valid, local_index, axis=0))[:, None]
    passage_grad = lax.psum_scatter(
        (inverse_temp * (block_term - own_rows)).astype(jnp.bfloat16),
        "dev",
        scatter_dimension=0,
        tiled=True,
    )
    joined = jnp.concatenate([query_grad, passage_grad], axis=1).reshape(
        n_all, capacity, 2 * width_d
    )
    returned_rows = route_back(joined).reshape(slots, 2 * width_d)
    unplaced = lax.dot_general(
        placer, returned_rows, (((0,), (0,)), ((), ())), preferred_element_type=jnp.float32
    ).astype(jnp.bfloat16)
    return (unplaced[:, :width_d], unplaced[:, width_d:])


def solution(mesh):
    placed = (P(("grp", "dev"), None), P(("grp", "dev"), None), P(("grp", "dev"), None))
    return jax.shard_map(
        local,
        mesh=mesh,
        in_specs=placed,
        out_specs=(P(("grp", "dev"), None), P(("grp", "dev"), None)),
        check_vma=False,
    )
```

profile of v0, /device:TPU:1, one launch (start us, length us, event | category | flops | bytes accessed | tf_op | source)
XLA Modules:
  0.0 389.4 jit_solution(12911759020453902526)
XLA Ops:
  7.2 0.0 all-gather.3.cloned.1.call-start
  7.2 0.9 convert_reduce_fusion.1
  8.1 0.7 multiply_add_fusion
  8.8 4.7 %convolution_convert_fusion = bf16[256,8192]{1,0:T(8,128)(2,1)} fusion(bf16[128,4096]{1,0:T(8,128)(2,1)} %param.4, bf16[128,4096]{1,0:T(8,128)(2,1)} %param.3, s32[128]{0:T(128)S(1)} %multiply_add_fusion), kind=kOutput, calls=%fused_computation.3 | convolution fusion | flops 543195136 | bytes 6291968 | tf_op jit(solution)/shard_map/dot_general | solution.py:35
  13.5 7.6 %reshape.80 = bf16[128,2,8192]{2,1,0:T(2,128)(2,1)} reshape(bf16[256,8192]{1,0:T(8,128)(2,1)} %convolution_convert_fusion) | data formatting | bytes 8388608 | tf_op jit(solution)/shard_map/reshape | solution.py:38
  21.1 64.7 %all_to_all.20 = bf16[128,2,8192]{2,1,0:T(2,128)(2,1)} all-to-all(bf16[128,2,8192]{2,1,0:T(2,128)(2,1)} %reshape.80), channel_id=1, replica_groups=mesh['grp'=16,'dev'=8] {'grp','dev'}, dimensions={0} | all-to-all | bytes 8388608 | tf_op jit(solution)/shard_map/all_to_all | solution.py:11
  85.8 7.2 %reshape.81 = bf16[256,8192]{1,0:T(8,128)(2,1)} reshape(bf16[128,2,8192]{2,1,0:T(2,128)(2,1)} %all_to_all.20) | data formatting | bytes 8388608 | tf_op jit(solution)/shard_map/reshape | solution.py:40
  93.0 4.0 %fusion.21 = (bf16[256,4096]{1,0:T(8,128)(2,1)}, bf16[256,4096]{1,0:T(8,128)(2,1)S(1)}) fusion(bf16[256,8192]{1,0:T(8,128)(2,1)} %reshape.81), kind=kLoop, calls=%fused_computation.42 | loop fusion | bytes 8388608 | tf_op jit(solution)/shard_map/slice | solution.py:44
  97.0 0.0 all-gather.3.cloned.1.call-update
  97.1 0.1 fusion.8
  97.2 0.8 all_to_all.16
  98.0 5.1 %all-to-all-start = ((bf16[128,1,2]{2,1,0:T(2,128)(2,1)}), bf16[128,1,2]{2,1,0:T(2,128)(2,1)S(1)}, u32[]{:S(2)}, u32[]{:S(2)}) async-start(bf16[128,1,2]{2,1,0:T(2,128)(2,1)} %all_to_all.16), calls=%async_computation | async-start | bytes 131072 | tf_op jit(solution)/shard_map/all_to_all | solution.py:12
  103.1 0.0 reduce-scatter.2.cloned.1.call-start
  103.3 9.2 %all-to-all-done = bf16[128,1,2]{2,1,0:T(2,128)(2,1)S(1)} async-done(((bf16[128,1,2]{2,1,0:T(2,128)(2,1)}), bf16[128,1,2]{2,1,0:T(2,128)(2,1)S(1)}, u32[]{:S(2)}, u32[]{:S(2)}) %all-to-all-start) | async-done | bytes 544 | tf_op jit(solution)/shard_map/all_to_all | solution.py:12
  112.4 0.2 reduce.1
  112.6 0.1 reshape.100
  112.8 10.1 %all-gather = bf16[8,1,256]{2,1,0:T(2,128)(2,1)S(1)} all-gather(bf16[1,1,256]{2,1,0:T(2,128)(2,1)S(1)} %reshape.100), channel_id=1, replica_groups=mesh['grp'=16,'dev'=8] {'dev'}, dimensions={0}, use_global_device_ids=true | all-gather | bytes 4608 | tf_op jit(solution)/shard_map/all_gather | solution.py:47
  122.9 0.2 convert_reduce_fusion
  123.1 0.1 reshape.106
  123.2 13.1 %gather_fusion.1 = f32[2048]{0:T(1024)S(1)} fusion(f32[256]{0:T(256)S(1)} %reshape.106, s32[2048]{0:T(1024)S(1)} %broadcast_clamp_fusion), kind=kCustom, calls=%fused_computation.1 | custom fusion | bytes 24576 | tf_op jit(solution)/shard_map/jit(_take)/gather | solution.py:73
  136.4 14.3 %gather_fusion = bf16[2048,4096]{1,0:T(8,128)(2,1)} fusion(bf16[256,4096]{1,0:T(8,128)(2,1)S(1)} %get-tuple-element.3, s32[2048]{0:T(1024)S(1)} %broadcast_clamp_fusion), kind=kCustom, calls=%fused_computation | custom fusion | bytes 33562624 | tf_op jit(solution)/shard_map/jit(_take)/gather | solution.py:72
  150.7 29.4 %all-gather.3.cloned.1.call-done = bf16[2048,4096]{1,0:T(8,128)(2,1)} async-done(((bf16[256,4096]{1,0:T(8,128)(2,1)}), bf16[2048,4096]{1,0:T(8,128)(2,1)}) %all-gather.3.cloned.1.call-update) | async-done | bytes 16777232 | tf_op jit(solution)/shard_map/all_gather | solution.py:46
  180.1 8.9 %fusion.23 = (f32[256]{0:T(256)S(1)}, f32[256,2048]{1,0:T(8,128)S(1)}) fusion(bf16[2048,4096]{1,0:T(8,128)(2,1)} %all-gather.3.cloned.1.call-done, bf16[256,8192]{1,0:T(8,128)(2,1)} %reshape.81, pred[2048]{0:T(1024)(128)(4,1)S(1)} %reshape.105), kind=kOutput, calls=%fused_computation.44 | convolution fusion | flops 4296540160 | bytes 20974592 | tf_op jit(solution)/shard_map/dot_general | solution.py:49
  189.0 0.4 fusion.6
  189.4 16.6 %multiply_convert_fusion = bf16[2048,4096]{1,0:T(8,128)(2,1)} fusion(f32[2048]{0:T(1024)S(1)} %select_select_fusion, bf16[2048,4096]{1,0:T(8,128)(2,1)} %gather_fusion, pred[2048]{0:T(1024)(128)(4,1)S(1)} %fusion.16, bf16[256,8192]{1,0:T(8,128)(2,1)} %reshape.81, f32[256,2048]{1,0:T(8,128)S(1)} %get-tuple-element.7, f32[256]{0:T(256)S(1)} %reshape.106, ...), kind=kOutput, calls=%fused_computation.2 | convolution fusion | flops 4347396096 | bytes 37762048 | tf_op jit(solution)/shard_map/dot_general | solution.py:66
  206.0 0.0 reduce-scatter.2.cloned.1.call-update
  206.0 12.5 %fusion.1 = bf16[256,4096]{1,0:T(8,128)(2,1)} fusion(bf16[2048,4096]{1,0:T(8,128)(2,1)} %all-gather.3.cloned.1.call-done, f32[256]{0:T(256)S(1)} %reshape.106, bf16[256,8192]{1,0:T(8,128)(2,1)} %reshape.81, f32[256,2048]{1,0:T(8,128)S(1)} %get-tuple-element.7, f32[256]{0:T(256)S(1)} %fusion.6, f32[256]{0:T(256)S(1)} %get-tuple-element.6), kind=kOutput, calls=%fused_computation.7 | convolution fusion | flops 4302307328 | bytes 23072768 | tf_op jit(solution)/shard_map/dot_general | solution.py:61
  218.6 78.5 %reduce-scatter.2.cloned.1.call-done = bf16[256,4096]{1,0:T(8,128)(2,1)} async-done(((bf16[2048,4096]{1,0:T(8,128)(2,1)}), bf16[256,4096]{1,0:T(8,128)(2,1)}) %reduce-scatter.2.cloned.1.call-update) | async-done | bytes 2097168 | tf_op jit(solution)/shard_map/reduce_scatter | solution.py:74
  297.0 4.6 %pad_maximum_fusion = bf16[256,8192]{1,0:T(8,128)(2,1)} fusion(bf16[256,4096]{1,0:T(8,128)(2,1)} %reduce-scatter.2.cloned.1.call-done, bf16[256,4096]{1,0:T(8,128)(2,1)} %fusion.1), kind=kLoop, calls=%fused_computation.8 | loop fusion | flops 8388608 | bytes 8388608 | tf_op jit(solution)/shard_map/concatenate | solution.py:80
  301.6 7.6 %reshape.82 = bf16[128,2,8192]{2,1,0:T(2,128)(2,1)} reshape(bf16[256,8192]{1,0:T(8,128)(2,1)} %pad_maximum_fusion) | data formatting | bytes 8388608 | tf_op jit(solution)/shard_map/reshape | solution.py:80
  309.3 61.6 %all_to_all.21 = bf16[128,2,8192]{2,1,0:T(2,128)(2,1)} all-to-all(bf16[128,2,8192]{2,1,0:T(2,128)(2,1)} %reshape.82), channel_id=1, replica_groups=mesh['grp'=16,'dev'=8] {'grp','dev'}, dimensions={0} | all-to-all | bytes 8388608 | tf_op jit(solution)/shard_map/all_to_all | solution.py:17
  370.8 7.2 %reshape.83 = bf16[256,8192]{1,0:T(8,128)(2,1)} reshape(bf16[128,2,8192]{2,1,0:T(2,128)(2,1)} %all_to_all.21) | data formatting | bytes 8388608 | tf_op jit(solution)/shard_map/reshape | solution.py:83
  378.0 2.9 convolution_convert_fusion.1
  381.0 1.5 fusion.22
  (6 shorter events, 0.1 us)
Async XLA Ops:
  7.2 172.9 %all-gather.3.cloned.1.call-start = ((), (), s32[]{:S(2)}) async-start(), calls=%async_computation.4 | async-start | bytes 18874368 | tf_op jit(solution)/shard_map/all_gather | solution.py:46
  98.0 14.5 %all-to-all-start = ((bf16[128,1,2]{2,1,0:T(2,128)(2,1)}), bf16[128,1,2]{2,1,0:T(2,128)(2,1)S(1)}, u32[]{:S(2)}, u32[]{:S(2)}) async-start(bf16[128,1,2]{2,1,0:T(2,128)(2,1)} %all_to_all.16), calls=%async_computation | async-start | bytes 131072 | tf_op jit(solution)/shard_map/all_to_all | solution.py:12
  103.1 193.9 %reduce-scatter.2.cloned.1.call-start = ((), (), s32[]{:S(2)}) async-start(), calls=%async_computation.5 | async-start | bytes 18874368 | tf_op jit(solution)/shard_map/reduce_scatter | solution.py:74
Sparse Core Ops, SparseCore 0:
  97.2 82.8 all-gather.2
  206.2 90.8 reduce-scatter.1
where the time goes:
time: 390 us; the launch traced here: 389 us
  blocking collectives  136 us (35%)
  waiting for transfers between devices  117 us (30%)
  local copies, waits for them, and re-layouts  63.8 us (16%)
  matrix products  45.7 us (12%)
  between operations  14.1 us (4%)
  other arithmetic  7.15 us (2%)
  starting transfers between devices  5.22 us (1%)
    reduce_scatter x1, waiting for transfers between devices, local(): lax.psum_scatter((inverse_temp * (block_term - own_rows)).astype(jnp.bflo...  78.5 us
    all_to_all x1, blocking collectives, route_out(): lax.all_to_all(payload, ('grp', 'dev'), split_axis=0, concat_axis=0, tile...  64.7 us
    all_to_all x1, blocking collectives, route_back(): lax.all_to_all(gradient_rows, ('grp', 'dev'), split_axis=0, concat_axis=0...  61.6 us
    all_gather x1, waiting for transfers between devices, local(): lax.all_gather(p_here, 'dev', axis=0, tiled=True)  29.4 us
    dot_general x1, matrix products, local(): lax.dot_general(softmax_bf, q_here, (((0,), (0,)), ((), ())), preferred_e...  16.6 us
    gather x1, local copies, waits for them, and re-layouts, local(): own_rows = jnp.take(q_here, local_index, axis=0).astype(jnp.float32)  14.3 us
    gather x1, local copies, waits for them, and re-layouts, local(): jnp.take(query_valid, local_index, axis=0)  13.1 us
    dot_general x1, matrix products, local(): jnp.dot(softmax_bf, p_all, preferred_element_type=jnp.float32)  12.5 us
  transfers between devices with their start and end apart: 3, of which 3 were waited for; matrix products, arithmetic and copies ran while one was open for 10% of the time, Pallas kernels for 0%

commit v1 on v0

v1 whole, which is shorter than its diff:
```python
import functools

import jax
import jax.numpy as jnp
from jax import lax
from jax.experimental import pallas as pl
from jax.experimental.pallas import tpu as pltpu
from jax.sharding import PartitionSpec as P

inverse_temp = 100.0
MESH = pl.DeviceIdType.MESH
SEATS = 32
NZ = 4
CHUNKS = 4
F32, BF16 = jnp.float32, jnp.bfloat16


def wait_bytes(ref, sem):
    pltpu.make_async_copy(ref, ref, sem).wait()


def kernel(
    drow_ref, q_ref, p_ref, oq_ref, op_ref,
    dest, xp, xq, place, unplace, pay_p, pay_q, p_all, q_rows, marks_out, marks, valid,
    scores, scores_in, soft, soft_t, dq, t1, t2, t3, ra, rb, rl, rr, dp, back_q, back_p, out_q, out_p,
    swap_s, swap_r, local_s, place_s, place_r, mark_s, mark_r, ring_s, ring_r, core_s, core_r,
    sum_s, sum_r, back_s, back_r, out_s, out_r,
):
    n_group = p_all.shape[2]
    npairs = q_ref.shape[0]
    half_d = q_ref.shape[1] // 2
    width = p_all.shape[4]
    rows = n_group * SEATS
    half_g = n_group // 2
    half = rows // 2
    g = lax.axis_index("grp")
    d = lax.axis_index("dev")
    c = lax.rem(d, 2)
    z = lax.div(d, 2)
    up = lax.rem(z + 1, NZ) * 2 + c
    down = lax.rem(z + NZ - 1, NZ) * 2 + c
    far = lax.rem(z + 2, NZ) * 2 + c
    mate = z * 2 + (1 - c)

    def remote(src, dst, s, r, to):
        return pltpu.make_async_remote_copy(
            src_ref=src, dst_ref=dst, send_sem=s, recv_sem=r, device_id=to, device_id_type=MESH
        )

    mine = pl.ds(pl.multiple_of(c * half_d, half_d), half_d)
    theirs = pl.ds(pl.multiple_of((1 - c) * half_d, half_d), half_d)
    own_copies = [
        pltpu.make_async_copy(drow_ref, dest.at[c], local_s.at[0]),
        pltpu.make_async_copy(p_ref.at[:, mine], xp.at[c], local_s.at[1]),
        pltpu.make_async_copy(q_ref.at[:, mine], xq.at[c], local_s.at[2]),
    ]
    for copy in own_copies:
        copy.start()

    barrier = pltpu.get_barrier_semaphore()
    for to in (up, down, far, mate):
        pl.semaphore_signal(barrier, inc=1, device_id=(g, to), device_id_type=MESH)

    @pl.loop(1, n_group)
    def _(o):
        pl.semaphore_signal(barrier, inc=1, device_id=(lax.rem(g + o, n_group), d), device_id_type=MESH)

    pl.semaphore_wait(barrier, n_group + 3)

    swaps = [
        remote(drow_ref, dest.at[c], swap_s.at[0], swap_r.at[0], (g, mate)),
        remote(p_ref.at[:, theirs], xp.at[c], swap_s.at[1], swap_r.at[1], (g, mate)),
        remote(q_ref.at[:, theirs], xq.at[c], swap_s.at[2], swap_r.at[2], (g, mate)),
    ]
    for copy in swaps:
        copy.start()

    own_copies[0].wait()
    swaps[0].wait_recv()
    n2 = 2 * npairs
    group = jnp.concatenate([dest[0, 0:1, :], dest[1, 0:1, :]], axis=1)
    group = lax.shift_right_logical(group, jnp.full_like(group, 3))
    along = jnp.broadcast_to(group.astype(F32), (n2, n2))
    across = along.T
    i0 = lax.broadcasted_iota(jnp.int32, (n2, n2), 0)
    i1 = lax.broadcasted_iota(jnp.int32, (n2, n2), 1)
    same = along == across
    rank_row = jnp.sum(jnp.where(same & (i0 < i1), 1.0, 0.0), axis=0, keepdims=True)
    rank_col = jnp.sum(jnp.where(same & (i1 < i0), 1.0, 0.0), axis=1, keepdims=True)
    slot_row = (group.astype(F32) * SEATS + rank_row).astype(jnp.int32)
    slot_col = (across[:, 0:1] * SEATS + rank_col).astype(jnp.int32)
    place[...] = jnp.where(
        lax.broadcasted_iota(jnp.int32, (rows, n2), 0) == slot_row, 1.0, 0.0
    ).astype(BF16)
    unplace[...] = jnp.where(
        lax.broadcasted_iota(jnp.int32, (n2, rows), 1) == slot_col, 1.0, 0.0
    ).astype(BF16)
    count = jnp.sum(
        jnp.where(lax.broadcasted_iota(jnp.int32, (n_group, n2), 0) == group, 1.0, 0.0), axis=1, keepdims=True
    ).astype(jnp.int32)
    lane = lax.broadcasted_iota(jnp.int32, (n_group, 128), 1) - lax.rem(g, 4) * SEATS
    flags = jnp.where((lane >= 0) & (lane < count), 1.0, 0.0)
    for i in range(n_group):
        marks_out[i] = jnp.broadcast_to(flags[i : i + 1], (8, 128))

    def send_all(src, dst, s, r):
        @pl.loop(1, n_group)
        def _(o):
            to = lax.rem(g + o, n_group)
            remote(src.at[to], dst.at[g], s, r, (to, d)).start()

    own_copies[1].wait()
    swaps[1].wait_recv()

    def place_p(k):
        cols = slice(k * width, (k + 1) * width)
        x = xp[:, :, cols].reshape(n2, width)
        pay_p[k] = jnp.dot(place[...], x, preferred_element_type=F32).astype(BF16).reshape(n_group, SEATS, width)
        send_all(pay_p.at[k], p_all.at[k, 0], place_s.at[0, k], place_r.at[0, k])
        p_all[k, 0, g] = pay_p[k, g]

    def place_q(k):
        cols = slice(k * width, (k + 1) * width)
        x = xq[:, :, cols].reshape(n2, width)
        pay_q[k] = jnp.dot(place[...], x, preferred_element_type=F32).astype(BF16).reshape(n_group, SEATS, width)
        send_all(pay_q.at[k], q_rows.at[k], place_s.at[1, k], place_r.at[1, k])
        q_rows[k, g] = pay_q[k, g]

    def wait_all(ref, sem):
        wait_bytes(ref.at[pl.ds(0, n_group - 1)], sem)

    place_p(0)
    send_all(marks_out, marks.at[0], mark_s.at[0], mark_r.at[0])
    marks[0, g] = marks_out[g]
    place_p(1)
    own_copies[2].wait()
    swaps[2].wait_recv()
    place_q(0)
    for k in range(2, CHUNKS):
        place_p(k)
        place_q(k - 1)
    place_q(CHUNKS - 1)

    lo, hi = pl.ds(0, half_g), pl.ds(half_g, half_g)

    def ring(k, i):
        own, above, beyond, below = (p_all.at[k, j] for j in range(4))
        src, dst, to = (
            (own.at[lo], below.at[lo], up),
            (own.at[hi], below.at[hi], up),
            (own.at[hi], above.at[hi], down),
            (own.at[lo], above.at[lo], down),
            (below.at[lo], beyond.at[lo], up),
            (above.at[hi], beyond.at[hi], down),
        )[i]
        return remote(src, dst, ring_s.at[k, i], ring_r.at[k, i], (g, to))

    def add_scores(k, j):
        part = lax.dot_general(
            q_rows[k].reshape(rows, width), p_all[k, j].reshape(rows, width),
            (((1,), (1,)), ((), ())), preferred_element_type=F32,
        )
        scores[j] = part if k == 0 else scores[j] + part

    mark_ring = [
        remote(marks.at[0], marks.at[3], mark_s.at[1], mark_r.at[1], (g, up)),
        remote(marks.at[0], marks.at[1], mark_s.at[2], mark_r.at[2], (g, down)),
        remote(marks.at[0], marks.at[2], mark_s.at[3], mark_r.at[3], (g, far)),
    ]

    for step in range(CHUNKS + 1):
        if step < CHUNKS:
            wait_all(p_all.at[step, 0], place_r.at[0, step])
            for i in (0, 2, 1, 3):
                ring(step, i).start()
        if step == 0:
            wait_all(marks.at[0], mark_r.at[0])
            for copy in mark_ring:
                copy.start()
        if step >= 1:
            k = step - 1
            ring(k, 0).wait_recv()
            ring(k, 4).start()
            ring(k, 2).wait_recv()
            ring(k, 5).start()
        if step == 1:
            for copy in mark_ring:
                copy.wait_recv()
            for j in range(NZ):
                pieces = []
                for first in range(0, n_group, 4):
                    flag = marks[j, first, 0:1, :]
                    for i in range(first + 1, min(first + 4, n_group)):
                        flag = flag + marks[j, i, 0:1, :]
                    pieces.append(flag)
                flag = pieces[0] if len(pieces) == 1 else jnp.concatenate(pieces, axis=1)
                valid[j] = jnp.broadcast_to(flag[:, :rows], (8, rows))
        if step >= 2:
            k = step - 2
            wait_all(q_rows.at[k], place_r.at[1, k])
            for i in (1, 3, 4, 5):
                ring(k, i).wait_recv()
            for j in range(NZ):
                add_scores(k, j)

    row_valid = jnp.broadcast_to(valid[0, 0:1, :], (128, rows)).T

    my_rows = pl.ds(pl.multiple_of(c * half, half), half)
    mate_rows = pl.ds(pl.multiple_of((1 - c) * half, half), half)

    def share(j):
        return remote(scores.at[j, mate_rows], scores_in.at[j], core_s.at[j], core_r.at[j], (g, mate))

    last = CHUNKS - 1
    wait_all(q_rows.at[last], place_r.at[1, last])
    for j in (0, 3, 1, 2):
        if j == 3:
            ring(last, 1).wait_recv()
        if j == 1:
            ring(last, 3).wait_recv()
        if j == 2:
            ring(last, 4).wait_recv()
            ring(last, 5).wait_recv()
        add_scores(last, j)
        share(j).start()

    out_q_cols = row_valid
    soft_t[0, :, 0:128] = out_q_cols.astype(BF16)
    for j in range(NZ):
        share(j).wait_recv()

    tile = min(16, half)

    @pl.loop(0, half // tile)
    def _(i):
        at_out = pl.ds(pl.multiple_of(c * half + i * tile, tile), tile)
        at_in = pl.ds(pl.multiple_of(i * tile, tile), tile)
        keep = soft_t[0, at_out, 0:1].astype(F32)
        parts = []
        top = None
        for j in range(NZ):
            s = inverse_temp * (scores[j, at_out, :] + scores_in[j, at_in, :])
            s = jnp.where(valid[j, 0:1, :] > 0, s, -1e30)
            parts.append(s)
            m = jnp.max(s, axis=1, keepdims=True)
            top = m if top is None else jnp.maximum(top, m)
        total = None
        exps = []
        for s in parts:
            e = jnp.exp(s - top)
            exps.append(e)
            t = jnp.sum(e, axis=1, keepdims=True)
            total = t if total is None else total + t
        for j in range(NZ):
            soft[j, at_out, :] = (exps[j] / total * keep).astype(BF16)

    give = remote(soft.at[:, my_rows], soft.at[:, my_rows], core_s.at[NZ], core_r.at[NZ], (g, mate))
    give.start()
    my_lanes = pl.ds(pl.multiple_of(c * half, half), half)
    mate_lanes = pl.ds(pl.multiple_of((1 - c) * half, half), half)
    for j in (2, 1, 3, 0):
        soft_t[j, :, my_lanes] = soft[j, my_rows, :].T
    give.wait_recv()
    for j in (2, 1, 3, 0):
        soft_t[j, :, mate_lanes] = soft[j, mate_rows, :].T

    def q_of(k):
        return q_rows[k].reshape(rows, width)

    def term(k, j, first, size):
        return inverse_temp * jnp.dot(soft_t[j, pl.ds(first, size), :], q_of(k), preferred_element_type=F32)

    a, b = pl.ds(0, half), pl.ds(half, half)

    def summed(k, i):
        src, dst, to = (
            (t2.at[k, a], ra.at[k], up),
            (t2.at[k, b], rb.at[k], down),
            (t1.at[k, b], rl.at[k, b], up),
            (t3.at[k, a], rr.at[k, a], down),
            (t1.at[k, a], rl.at[k, a], up),
            (t3.at[k, b], rr.at[k, b], down),
        )[i]
        return remote(src, dst, sum_s.at[k, i], sum_r.at[k, i], (g, to))

    for step in range(CHUNKS + 2):
        if step < CHUNKS:
            k = step
            t2[k] = term(k, 2, 0, rows).astype(BF16)
            summed(k, 0).start()
            summed(k, 1).start()
            t1[k, b] = term(k, 1, half, half).astype(BF16)
            summed(k, 2).start()
            t3[k, a] = term(k, 3, 0, half).astype(BF16)
            summed(k, 3).start()
        if 1 <= step <= CHUNKS:
            k = step - 1
            summed(k, 0).wait_recv()
            t1[k, a] = (term(k, 1, 0, half) + ra[k].astype(F32)).astype(BF16)
            summed(k, 4).start()
            summed(k, 1).wait_recv()
            t3[k, b] = (term(k, 3, half, half) + rb[k].astype(F32)).astype(BF16)
            summed(k, 5).start()
        if step < CHUNKS:
            k = step
            acc = -p_all[k, 0].reshape(rows, width).astype(F32)
            for j in range(NZ):
                acc = acc + jnp.dot(soft[j], p_all[k, j].reshape(rows, width), preferred_element_type=F32)
            dq[k] = (inverse_temp * acc).astype(BF16).reshape(n_group, SEATS, width)
            send_all(dq.at[k], back_q.at[k], back_s.at[0, k], back_r.at[0, k])
            back_q[k, g] = dq[k, g]
        if step >= 2:
            k = step - 2
            own = inverse_temp * (
                jnp.dot(soft_t[0], q_of(k), preferred_element_type=F32) - q_of(k).astype(F32)
            )
            for i in (2, 3, 4, 5):
                summed(k, i).wait_recv()
            own = own + rl[k].astype(F32) + rr[k].astype(F32)
            dp[k] = own.astype(BF16).reshape(n_group, SEATS, width)
            send_all(dp.at[k], back_p.at[k], back_s.at[1, k], back_r.at[1, k])
            back_p[k, g] = dp[k, g]

    def finish(k, which):
        back, out, o_ref = ((back_q, out_q, oq_ref), (back_p, out_p, op_ref))[which]
        wait_all(back.at[k], back_r.at[which, k])
        out[k] = (
            jnp.dot(unplace[...], back[k].reshape(rows, width), preferred_element_type=F32)
            .astype(BF16)
            .reshape(2, npairs, width)
        )
        here, there = outputs(k, which)
        here.start()
        there.start()

    def outputs(k, which):
        out, o_ref = ((out_q, oq_ref), (out_p, op_ref))[which]
        cols = pl.ds(pl.multiple_of(c * half_d + k * width, width), width)
        return (
            pltpu.make_async_copy(out.at[k, c], o_ref.at[:, cols], local_s.at[3 + which * CHUNKS + k]),
            remote(out.at[k, 1 - c], o_ref.at[:, cols], out_s.at[which, k], out_r.at[which, k], (g, mate)),
        )

    for k in range(CHUNKS):
        finish(k, 0)
    for k in range(CHUNKS):
        finish(k, 1)

    for copy in swaps:
        copy.wait_send()
    for k in range(CHUNKS):
        wait_all(pay_p.at[k], place_s.at[0, k])
        wait_all(pay_q.at[k], place_s.at[1, k])
        wait_all(dq.at[k], back_s.at[0, k])
        wait_all(dp.at[k], back_s.at[1, k])
        for i in range(6):
            ring(k, i).wait_send()
            summed(k, i).wait_send()
    wait_all(marks_out, mark_s.at[0])
    for copy in mark_ring:
        copy.wait_send()
    for j in range(NZ):
        share(j).wait_send()
    give.wait_send()
    for which in range(2):
        for k in range(CHUNKS):
            here, there = outputs(k, which)
            here.wait()
            there.wait()


def local(queries, passages, destination):
    n_group = lax.axis_size("grp")
    npairs, width_d = queries.shape
    half_d = width_d // 2
    width = half_d // CHUNKS
    rows = n_group * SEATS
    half = rows // 2
    drow = jnp.broadcast_to(destination.reshape(1, npairs), (8, npairs))
    dma = pltpu.SemaphoreType.DMA

    def vm(*shape, dtype=BF16):
        return pltpu.VMEM(shape, dtype)

    scratch = [
        vm(2, 8, npairs, dtype=jnp.int32),
        vm(2, npairs, half_d), vm(2, npairs, half_d),
        vm(rows, 2 * npairs), vm(2 * npairs, rows),
        vm(CHUNKS, n_group, SEATS, width), vm(CHUNKS, n_group, SEATS, width),
        vm(CHUNKS, NZ, n_group, SEATS, width), vm(CHUNKS, n_group, SEATS, width),
        vm(n_group, 8, 128, dtype=F32), vm(NZ, n_group, 8, 128, dtype=F32), vm(NZ, 8, rows, dtype=F32),
        vm(NZ, rows, rows, dtype=F32), vm(NZ, half, rows, dtype=F32),
        vm(NZ, rows, rows), vm(NZ, rows, rows),
        vm(CHUNKS, n_group, SEATS, width),
        vm(CHUNKS, rows, width), vm(CHUNKS, rows, width), vm(CHUNKS, rows, width),
        vm(CHUNKS, half, width), vm(CHUNKS, half, width),
        vm(CHUNKS, rows, width), vm(CHUNKS, rows, width),
        vm(CHUNKS, n_group, SEATS, width),
        vm(CHUNKS, n_group, SEATS, width), vm(CHUNKS, n_group, SEATS, width),
        vm(CHUNKS, 2, npairs, width), vm(CHUNKS, 2, npairs, width),
        dma((3,)), dma((3,)), dma((3 + 2 * CHUNKS,)),
        dma((2, CHUNKS)), dma((2, CHUNKS)), dma((4,)), dma((4,)),
        dma((CHUNKS, 6)), dma((CHUNKS, 6)), dma((NZ + 1,)), dma((NZ + 1,)),
        dma((CHUNKS, 6)), dma((CHUNKS, 6)), dma((2, CHUNKS)), dma((2, CHUNKS)),
        dma((2, CHUNKS)), dma((2, CHUNKS)),
    ]
    anywhere = pl.BlockSpec(memory_space=pl.ANY)
    return pl.pallas_call(
        kernel,
        out_shape=(
            jax.ShapeDtypeStruct((npairs, width_d), BF16),
            jax.ShapeDtypeStruct((npairs, width_d), BF16),
        ),
        in_specs=[pl.BlockSpec(memory_space=pltpu.VMEM), anywhere, anywhere],
        out_specs=(anywhere, anywhere),
        scratch_shapes=scratch,
        compiler_params=pltpu.CompilerParams(
            collective_id=0, has_side_effects=True, vmem_limit_bytes=67043328
        ),
    )(drow, queries, passages)


def solution(mesh):
    placed = (P(("grp", "dev"), None), P(("grp", "dev"), None), P(("grp", "dev"), None))
    return jax.shard_map(
        local,
        mesh=mesh,
        in_specs=placed,
        out_specs=(P(("grp", "dev"), None), P(("grp", "dev"), None)),
        check_vma=False,
    )
```

time: 390 us -> 198 us (0.51)
  Pallas kernels: 0 us -> 191 us
  blocking collectives: 136 us -> 0 us
  waiting for transfers between devices: 117 us -> 0 us
  local copies, waits for them, and re-layouts: 63.8 us -> 4.59 us
  matrix products: 45.7 us -> 0 us
  between operations: 14.1 us -> 0.66 us
  other arithmetic: 7.15 us -> 0 us
  starting transfers between devices: 5.22 us -> 0 us
    pallas_call x0 -> x1, Pallas kernels: none -> 191 us  [local(): pl.pallas_call(kernel, out_shape=(jax.ShapeDtypeStruct((npairs, width_d),...]
    all_to_all x2 -> x0, blocking collectives: 126 us -> none  [the longest x1 64.7 us: route_out(): lax.all_to_all(payload, ('grp', 'dev'), split_axis=0, concat_axis=0, tile...]
    reduce_scatter x1 -> x0, waiting for transfers between devices: 78.5 us -> none  [local(): lax.psum_scatter((inverse_temp * (block_term - own_rows)).astype(jnp.bflo...]
    dot_general x5 -> x0, matrix products: 45.7 us -> none  [the longest x1 16.6 us: local(): lax.dot_general(softmax_bf, q_here, (((0,), (0,)), ((), ())), preferred_e...]
    reshape x4 -> x0, local copies, waits for them, and re-layouts: 29.7 us -> none  [the longest x1 7.62 us: local(): jnp.concatenate([query_grad, passage_grad], axis=1)]
    all_gather x1 -> x0, waiting for transfers between devices: 29.4 us -> none  [local(): lax.all_gather(p_here, 'dev', axis=0, tiled=True)]
    gather x2 -> x0, local copies, waits for them, and re-layouts: 27.5 us -> none  [the longest x1 14.3 us: local(): own_rows = jnp.take(q_here, local_index, axis=0).astype(jnp.float32)]
    all_gather x1 -> x0, blocking collectives: 10.1 us -> none  [local(): lax.all_gather(slot_marks, 'dev', axis=0, tiled=True)]
  transfers between devices with their start and end apart: 3 -> 0, of which waited for: 3 -> 0; matrix products, arithmetic and copies ran while one was open for 10% -> 0% of each run, Pallas kernels for 0% -> 0%
where the time goes in v1:
time: 198 us; the launch traced here: 196 us
  Pallas kernels  191 us (96%)
  local copies, waits for them, and re-layouts  4.59 us (2%)
    pallas_call x1, Pallas kernels, local(): pl.pallas_call(kernel, out_shape=(jax.ShapeDtypeStruct((npairs, width_d),...  191 us
    unnamed x6, local copies, waits for them, and re-layouts  4 us

profile of v1, /device:TPU:1, one launch (start us, length us, event | category | flops | bytes accessed | tf_op | source)
XLA Modules:
  0.0 196.4 jit_solution(17837116265979187219)
XLA Ops:
  0.6 0.0 copy-start.1
  0.6 0.6 copy-done.1
  1.3 0.6 broadcast_in_dim.8.drow_ref
  1.9 191.2 %shard_map.50 = (bf16[128,4096]{1,0:T(8,128)(2,1)}, bf16[128,4096]{1,0:T(8,128)(2,1)}) custom-call(s32[8,128]{1,0:T(8,128)} %broadcast_in_dim.8.drow_ref, bf16[128,4096]{1,0:T(8,128)(2,1)} %q_ref.1, bf16[128,4096]{1,0:T(8,128)(2,1)} %p_ref.1), custom_call_target="tpu_custom_call" | custom-call | tf_op jit(solution)/shard_map/pallas_call | solution.py:408
  193.1 0.0 copy-start
  193.1 2.4 %copy.7 = bf16[128,4096]{1,0:T(8,128)(2,1)} copy(bf16[128,4096]{1,0:T(8,128)(2,1)} %get-tuple-element.4) | data formatting | bytes 2097152
  195.4 0.0 copy-done
  195.4 1.0 copy.8
Async XLA Ops:
  0.6 0.7 copy-start.1
  193.1 2.4 %copy-start = (bf16[128,4096]{1,0:T(8,128)(2,1)S(1)}, bf16[128,4096]{1,0:T(8,128)(2,1)}, u32[]{:S(2)}) copy-start(bf16[128,4096]{1,0:T(8,128)(2,1)} %get-tuple-element.5) | copy-start | bytes 3145732

commit v2 on v0

v2 whole, which is shorter than its diff:
```python
import functools

import jax
import jax.numpy as jnp
from jax import lax
from jax.experimental import pallas as pl
from jax.experimental.pallas import tpu as pltpu
from jax.sharding import PartitionSpec as P

inverse_temp = 100.0
MESH = pl.DeviceIdType.MESH
SEATS = 32
FEW = 24
NZ = 4
CHUNKS = 8
F32, BF16 = jnp.float32, jnp.bfloat16


def wait_bytes(ref, sem):
    pltpu.make_async_copy(ref, ref, sem).wait()


def remote(src, dst, s, r, to):
    return pltpu.make_async_remote_copy(
        src_ref=src, dst_ref=dst, send_sem=s, recv_sem=r, device_id=to, device_id_type=MESH
    )


def where_am_i():
    g = lax.axis_index("grp")
    d = lax.axis_index("dev")
    c = lax.rem(d, 2)
    z = lax.div(d, 2)
    up = lax.rem(z + 1, NZ) * 2 + c
    down = lax.rem(z + NZ - 1, NZ) * 2 + c
    far = lax.rem(z + 2, NZ) * 2 + c
    mate = z * 2 + (1 - c)
    return g, d, c, up, down, far, mate


def greet(n_group):
    g, d, c, up, down, far, mate = where_am_i()
    barrier = pltpu.get_barrier_semaphore()
    for to in (up, down, far, mate):
        pl.semaphore_signal(barrier, inc=1, device_id=(g, to), device_id_type=MESH)

    @pl.loop(1, n_group)
    def _(o):
        pl.semaphore_signal(barrier, inc=1, device_id=(lax.rem(g + o, n_group), d), device_id_type=MESH)

    return lambda: pl.semaphore_wait(barrier, n_group + 3)


def first_kernel(
    drow_ref, q_ref, p_ref, pay_p_ref, pay_q_ref, marks_ref, unplace_ref, top_ref,
    dest, xp, xq, place, pay_p, pay_q, own_top, tops, plane_top, plane_tops,
    swap_s, swap_r, local_s, keep_s, top_s, top_r, plane_s, plane_r,
):
    n_group = pay_p.shape[1]
    npairs = q_ref.shape[0]
    half_d = q_ref.shape[1] // 2
    width = pay_p.shape[3]
    rows = n_group * SEATS
    g, d, c, up, down, far, mate = where_am_i()

    mine = pl.ds(pl.multiple_of(c * half_d, half_d), half_d)
    theirs = pl.ds(pl.multiple_of((1 - c) * half_d, half_d), half_d)
    own_copies = [
        pltpu.make_async_copy(drow_ref, dest.at[c], local_s.at[0]),
        pltpu.make_async_copy(p_ref.at[:, mine], xp.at[c], local_s.at[1]),
        pltpu.make_async_copy(q_ref.at[:, mine], xq.at[c], local_s.at[2]),
    ]
    for copy in own_copies:
        copy.start()
    greet(n_group)()
    swaps = [
        remote(drow_ref, dest.at[c], swap_s.at[0], swap_r.at[0], (g, mate)),
        remote(p_ref.at[:, theirs], xp.at[c], swap_s.at[1], swap_r.at[1], (g, mate)),
        remote(q_ref.at[:, theirs], xq.at[c], swap_s.at[2], swap_r.at[2], (g, mate)),
    ]
    for copy in swaps:
        copy.start()

    own_copies[0].wait()
    swaps[0].wait_recv()
    n2 = 2 * npairs
    group = jnp.concatenate([dest[0, 0:1, :], dest[1, 0:1, :]], axis=1)
    group = lax.shift_right_logical(group, jnp.full_like(group, 3))
    count = jnp.sum(
        jnp.where(lax.broadcasted_iota(jnp.int32, (n_group, n2), 0) == group, 1.0, 0.0), axis=1, keepdims=True
    )
    own_top[...] = jnp.broadcast_to(jnp.max(count, axis=0, keepdims=True), (8, 128))
    tops[g] = own_top[...]

    @pl.loop(1, n_group)
    def _(o):
        to = lax.rem(g + o, n_group)
        remote(own_top, tops.at[g], top_s, top_r, (to, d)).start()

    along = jnp.broadcast_to(group.astype(F32), (n2, n2))
    across = along.T
    i0 = lax.broadcasted_iota(jnp.int32, (n2, n2), 0)
    i1 = lax.broadcasted_iota(jnp.int32, (n2, n2), 1)
    same = along == across
    rank_row = jnp.sum(jnp.where(same & (i0 < i1), 1.0, 0.0), axis=0, keepdims=True)
    rank_col = jnp.sum(jnp.where(same & (i1 < i0), 1.0, 0.0), axis=1, keepdims=True)
    slot_row = (group.astype(F32) * SEATS + rank_row).astype(jnp.int32)
    slot_col = (across[:, 0:1] * SEATS + rank_col).astype(jnp.int32)
    place[...] = jnp.where(
        lax.broadcasted_iota(jnp.int32, (rows, n2), 0) == slot_row, 1.0, 0.0
    ).astype(BF16)
    unplace_ref[...] = jnp.where(
        lax.broadcasted_iota(jnp.int32, (n2, rows), 1) == slot_col, 1.0, 0.0
    ).astype(BF16)
    lane = lax.broadcasted_iota(jnp.int32, (n_group, 128), 1) - lax.rem(g, 4) * SEATS
    flags = jnp.where((lane >= 0) & (lane < count.astype(jnp.int32)), 1.0, 0.0)
    for i in range(n_group):
        marks_ref[i] = jnp.broadcast_to(flags[i : i + 1], (8, 128))

    def fill(x, pay, pay_ref, which):
        @pl.loop(0, CHUNKS)
        def _(k):
            cols = pl.ds(pl.multiple_of(k * width, width), width)
            part = jnp.dot(place[...], x[:, :, cols].reshape(n2, width), preferred_element_type=F32)
            pay[k] = part.astype(BF16).reshape(n_group, SEATS, width)
            pltpu.make_async_copy(pay.at[k], pay_ref.at[k], keep_s.at[which, k]).start()

    own_copies[1].wait()
    swaps[1].wait_recv()
    fill(xp, pay_p, pay_p_ref, 0)

    wait_bytes(tops.at[pl.ds(0, n_group - 1)], top_r)
    top = tops[0]
    for i in range(1, n_group):
        top = jnp.maximum(top, tops[i])
    plane_top[...] = top
    plane_copies = [
        remote(plane_top, plane_tops.at[i], plane_s.at[i], plane_r.at[i], (g, to))
        for i, to in enumerate((up, down, far))
    ]
    for copy in plane_copies:
        copy.start()

    own_copies[2].wait()
    swaps[2].wait_recv()
    fill(xq, pay_q, pay_q_ref, 1)

    for copy in plane_copies:
        copy.wait_recv()
    top_ref[...] = jnp.maximum(
        jnp.maximum(plane_top[...], plane_tops[0]), jnp.maximum(plane_tops[1], plane_tops[2])
    )
    for copy in swaps:
        copy.wait_send()
    for copy in plane_copies:
        copy.wait_send()
    wait_bytes(tops.at[pl.ds(0, n_group - 1)], top_s)

    @pl.loop(0, CHUNKS)
    def _(k):
        pltpu.make_async_copy(pay_p.at[k], pay_p_ref.at[k], keep_s.at[0, k]).wait()
        pltpu.make_async_copy(pay_q.at[k], pay_q_ref.at[k], keep_s.at[1, k]).wait()


def second_kernel(
    seats,
    pay_p, pay_q, marks_out, unplace, oq_ref, op_ref,
    p_all, q_rows, marks, valid, scores, scores_in, soft, soft_t, dq, t1, t2, t3, ra, rb, rl, rr, dp,
    back_q, back_p, out_q, out_p,
    local_s, place_s, place_r, mark_s, mark_r, ring_s, ring_r, core_s, core_r,
    sum_s, sum_r, back_s, back_r, keep_s, out_s, out_r,
):
    n_group = p_all.shape[2]
    npairs, width_d = oq_ref.shape
    half_d = width_d // 2
    width = p_all.shape[4]
    rows = n_group * SEATS
    half_g = n_group // 2
    half = rows // 2
    g, d, c, up, down, far, mate = where_am_i()
    taken = pl.ds(0, seats)

    ready = greet(n_group)
    if seats < SEATS:
        rest = slice(seats, SEATS)
        empty = jnp.zeros((n_group, SEATS - seats, width), BF16)

        @pl.loop(0, CHUNKS)
        def _(k):
            for j in range(NZ):
                p_all[k, j, :, rest, :] = empty
            for ref in (q_rows, back_q, back_p):
                ref[k, :, rest, :] = empty

    ready()

    def send_all(src, dst, s, r):
        @pl.loop(1, n_group)
        def _(o):
            to = lax.rem(g + o, n_group)
            remote(src.at[to, taken], dst.at[g, taken], s, r, (to, d)).start()

    def wait_all(ref, sem):
        wait_bytes(ref.at[pl.ds(0, n_group - 1), taken], sem)

    def send_p(k):
        send_all(pay_p.at[k], p_all.at[k, 0], place_s.at[0, k], place_r.at[0, k])

    own_copies = [
        pltpu.make_async_copy(pay_p.at[:, g, taken], p_all.at[:, 0, g, taken], local_s.at[0]),
        pltpu.make_async_copy(pay_q.at[:, g, taken], q_rows.at[:, g, taken], local_s.at[1]),
        pltpu.make_async_copy(marks_out.at[g], marks.at[0, g], local_s.at[2]),
    ]
    send_p(0)
    for copy in own_copies:
        copy.start()

    @pl.loop(1, n_group)
    def _(o):
        to = lax.rem(g + o, n_group)
        remote(marks_out.at[to], marks.at[0, g], mark_s.at[0], mark_r.at[0], (to, d)).start()

    @pl.loop(1, CHUNKS)
    def _(k):
        send_p(k)

    @pl.loop(0, CHUNKS)
    def _(k):
        send_all(pay_q.at[k], q_rows.at[k], place_s.at[1, k], place_r.at[1, k])

    lo, hi = pl.ds(0, half_g), pl.ds(half_g, half_g)

    def ring(k, i):
        own, above, beyond, below = (p_all.at[k, j] for j in range(4))
        src, dst, part, to = (
            (own, below, lo, up),
            (own, below, hi, up),
            (own, above, hi, down),
            (own, above, lo, down),
            (below, beyond, lo, up),
            (above, beyond, hi, down),
        )[i]
        return remote(src.at[part, taken], dst.at[part, taken], ring_s.at[k, i], ring_r.at[k, i], (g, to))

    def score_part(k, j):
        return lax.dot_general(
            q_rows[k].reshape(rows, width), p_all[k, j].reshape(rows, width),
            (((1,), (1,)), ((), ())), preferred_element_type=F32,
        )

    def start_ring(k):
        wait_all(p_all.at[k, 0], place_r.at[0, k])
        for i in (0, 2, 1, 3):
            ring(k, i).start()

    def pass_on(k):
        ring(k, 0).wait_recv()
        ring(k, 4).start()
        ring(k, 2).wait_recv()
        ring(k, 5).start()

    def add_scores(k):
        wait_all(q_rows.at[k], place_r.at[1, k])
        for i in (1, 3, 4, 5):
            ring(k, i).wait_recv()

        @pl.loop(0, NZ)
        def _(j):
            scores[j] = scores[j] + score_part(k, j)

    mark_ring = [
        remote(marks.at[0], marks.at[3], mark_s.at[1], mark_r.at[1], (g, up)),
        remote(marks.at[0], marks.at[1], mark_s.at[2], mark_r.at[2], (g, down)),
        remote(marks.at[0], marks.at[2], mark_s.at[3], mark_r.at[3], (g, far)),
    ]

    for copy in own_copies:
        copy.wait()
    start_ring(0)
    wait_bytes(marks.at[0, pl.ds(0, n_group - 1)], mark_r.at[0])
    for copy in mark_ring:
        copy.start()
    start_ring(1)
    pass_on(0)
    scores[...] = jnp.zeros_like(scores)
    for copy in mark_ring:
        copy.wait_recv()
    for j in range(NZ):
        pieces = []
        for first in range(0, n_group, 4):
            flag = marks[j, first, 0:1, :]
            for i in range(first + 1, min(first + 4, n_group)):
                flag = flag + marks[j, i, 0:1, :]
            pieces.append(flag)
        flag = pieces[0] if len(pieces) == 1 else jnp.concatenate(pieces, axis=1)
        valid[j] = jnp.broadcast_to(flag[:, :rows], (8, rows))
    soft_t[0, :, 0:128] = jnp.broadcast_to(valid[0, 0:1, :], (128, rows)).T.astype(BF16)

    @pl.loop(2, CHUNKS)
    def _(step):
        start_ring(step)
        pass_on(step - 1)
        add_scores(step - 2)

    pass_on(CHUNKS - 1)
    add_scores(CHUNKS - 2)

    my_rows = pl.ds(pl.multiple_of(c * half, half), half)
    mate_rows = pl.ds(pl.multiple_of((1 - c) * half, half), half)

    def share(j):
        return remote(scores.at[j, mate_rows], scores_in.at[j], core_s.at[j], core_r.at[j], (g, mate))

    last = CHUNKS - 1
    wait_all(q_rows.at[last], place_r.at[1, last])
    for j, needs in ((0, ()), (3, (1,)), (1, (3,)), (2, (4, 5))):
        for i in needs:
            ring(last, i).wait_recv()
        scores[j] = scores[j] + score_part(last, j)
        share(j).start()
    for j in range(NZ):
        share(j).wait_recv()

    tile = min(16, half)

    @pl.loop(0, half // tile)
    def _(i):
        at_out = pl.ds(pl.multiple_of(c * half + i * tile, tile), tile)
        at_in = pl.ds(pl.multiple_of(i * tile, tile), tile)
        keep = soft_t[0, at_out, 0:1].astype(F32)
        parts = []
        top = None
        for j in range(NZ):
            s = inverse_temp * (scores[j, at_out, :] + scores_in[j, at_in, :])
            s = jnp.where(valid[j, 0:1, :] > 0, s, -1e30)
            parts.append(s)
            m = jnp.max(s, axis=1, keepdims=True)
            top = m if top is None else jnp.maximum(top, m)
        total = None
        exps = []
        for s in parts:
            e = jnp.exp(s - top)
            exps.append(e)
            t = jnp.sum(e, axis=1, keepdims=True)
            total = t if total is None else total + t
        for j in range(NZ):
            soft[j, at_out, :] = (exps[j] / total * keep).astype(BF16)

    give = remote(soft.at[:, my_rows], soft.at[:, my_rows], core_s.at[NZ], core_r.at[NZ], (g, mate))
    give.start()
    my_lanes = pl.ds(pl.multiple_of(c * half, half), half)
    mate_lanes = pl.ds(pl.multiple_of((1 - c) * half, half), half)

    @pl.loop(0, NZ)
    def _(j):
        soft_t[j, :, my_lanes] = soft[j, my_rows, :].T

    give.wait_recv()

    @pl.loop(0, NZ)
    def _(j):
        soft_t[j, :, mate_lanes] = soft[j, mate_rows, :].T

    def q_of(k):
        return q_rows[k].reshape(rows, width)

    def term(k, j, first, size):
        return inverse_temp * jnp.dot(soft_t[j, pl.ds(first, size), :], q_of(k), preferred_element_type=F32)

    def blocks(x):
        return x.astype(BF16).reshape(x.shape[0] // SEATS, SEATS, width)

    def summed(k, i):
        src, dst, to = (
            (t2.at[k, lo, taken], ra.at[k, :, taken], up),
            (t2.at[k, hi, taken], rb.at[k, :, taken], down),
            (t1.at[k, hi, taken], rl.at[k, hi, taken], up),
            (t3.at[k, lo, taken], rr.at[k, lo, taken], down),
            (t1.at[k, lo, taken], rl.at[k, lo, taken], up),
            (t3.at[k, hi, taken], rr.at[k, hi, taken], down),
        )[i]
        return remote(src, dst, sum_s.at[k, i], sum_r.at[k, i], (g, to))

    def open_sums(k):
        t2[k] = blocks(term(k, 2, 0, rows))
        summed(k, 0).start()
        summed(k, 1).start()
        t1[k, hi] = blocks(term(k, 1, half, half))
        summed(k, 2).start()
        t3[k, lo] = blocks(term(k, 3, 0, half))
        summed(k, 3).start()

    def add_sums(k):
        summed(k, 0).wait_recv()
        t1[k, lo] = blocks(term(k, 1, 0, half) + ra[k].reshape(half, width).astype(F32))
        summed(k, 4).start()
        summed(k, 1).wait_recv()
        t3[k, hi] = blocks(term(k, 3, half, half) + rb[k].reshape(half, width).astype(F32))
        summed(k, 5).start()

    def query_part(k):
        acc = -p_all[k, 0].reshape(rows, width).astype(F32)
        for j in range(NZ):
            acc = acc + jnp.dot(soft[j], p_all[k, j].reshape(rows, width), preferred_element_type=F32)
        dq[k] = blocks(inverse_temp * acc)
        send_all(dq.at[k], back_q.at[k], back_s.at[0, k], back_r.at[0, k])
        back_q[k, g, 0:seats] = dq[k, g, 0:seats]

    def close_sums(k):
        own = inverse_temp * (
            jnp.dot(soft_t[0], q_of(k), preferred_element_type=F32) - q_of(k).astype(F32)
        )
        for i in (2, 3, 4, 5):
            summed(k, i).wait_recv()
        own = own + rl[k].reshape(rows, width).astype(F32) + rr[k].reshape(rows, width).astype(F32)
        dp[k] = blocks(own)
        send_all(dp.at[k], back_p.at[k], back_s.at[1, k], back_r.at[1, k])
        back_p[k, g, 0:seats] = dp[k, g, 0:seats]

    open_sums(0)
    query_part(0)
    open_sums(1)
    add_sums(0)
    query_part(1)

    @pl.loop(2, CHUNKS)
    def _(k):
        open_sums(k)
        add_sums(k - 1)
        query_part(k)
        close_sums(k - 2)

    add_sums(CHUNKS - 1)
    close_sums(CHUNKS - 2)
    close_sums(CHUNKS - 1)

    def outputs(k, which):
        out, o_ref = ((out_q, oq_ref), (out_p, op_ref))[which]
        cols = pl.ds(pl.multiple_of(c * half_d + k * width, width), width)
        return (
            pltpu.make_async_copy(out.at[k, c], o_ref.at[:, cols], keep_s.at[which, k]),
            remote(out.at[k, 1 - c], o_ref.at[:, cols], out_s.at[which, k], out_r.at[which, k], (g, mate)),
        )

    for which in range(2):
        back, out = ((back_q, out_q), (back_p, out_p))[which]

        @pl.loop(0, CHUNKS)
        def _(k):
            wait_all(back.at[k], back_r.at[which, k])
            part = jnp.dot(unplace[...], back[k].reshape(rows, width), preferred_element_type=F32)
            out[k] = part.astype(BF16).reshape(2, npairs, width)
            here, there = outputs(k, which)
            here.start()
            there.start()

    @pl.loop(0, CHUNKS)
    def _(k):
        wait_all(pay_p.at[k], place_s.at[0, k])
        wait_all(pay_q.at[k], place_s.at[1, k])
        wait_all(dq.at[k], back_s.at[0, k])
        wait_all(dp.at[k], back_s.at[1, k])
        for i in range(6):
            ring(k, i).wait_send()
            summed(k, i).wait_send()
        for which in range(2):
            here, there = outputs(k, which)
            here.wait()
            there.wait()

    wait_bytes(marks_out.at[pl.ds(0, n_group - 1)], mark_s.at[0])
    for copy in mark_ring:
        copy.wait_send()
    for j in range(NZ):
        share(j).wait_send()
    give.wait_send()


def local(queries, passages, destination):
    n_group = lax.axis_size("grp")
    npairs, width_d = queries.shape
    half_d = width_d // 2
    width = half_d // CHUNKS
    rows = n_group * SEATS
    half = rows // 2
    half_g = n_group // 2
    drow = jnp.broadcast_to(destination.reshape(1, npairs), (8, npairs))
    dma = pltpu.SemaphoreType.DMA
    in_vmem = pl.BlockSpec(memory_space=pltpu.VMEM)
    anywhere = pl.BlockSpec(memory_space=pl.ANY)

    def vm(*shape, dtype=BF16):
        return pltpu.VMEM(shape, dtype)

    tile = (8, 128)
    payload = (CHUNKS, n_group, SEATS, width)
    pay_p, pay_q, marks, unplace, top = pl.pallas_call(
        first_kernel,
        out_shape=(
            jax.ShapeDtypeStruct(payload, BF16),
            jax.ShapeDtypeStruct(payload, BF16),
            jax.ShapeDtypeStruct((n_group, *tile), F32),
            jax.ShapeDtypeStruct((2 * npairs, rows), BF16),
            jax.ShapeDtypeStruct(tile, F32),
        ),
        in_specs=[in_vmem, anywhere, anywhere],
        out_specs=(anywhere, anywhere, in_vmem, in_vmem, in_vmem),
        scratch_shapes=[
            vm(2, 8, npairs, dtype=jnp.int32),
            vm(2, npairs, half_d), vm(2, npairs, half_d),
            vm(rows, 2 * npairs),
            vm(*payload), vm(*payload),
            vm(*tile, dtype=F32), vm(n_group, *tile, dtype=F32),
            vm(*tile, dtype=F32), vm(3, *tile, dtype=F32),
            dma((3,)), dma((3,)), dma((3,)), dma((2, CHUNKS)), dma(()), dma(()), dma((3,)), dma((3,)),
        ],
        compiler_params=pltpu.CompilerParams(collective_id=0, has_side_effects=True),
    )(drow, queries, passages)

    def rest(seats, collective_id):
        scratch = [
            vm(CHUNKS, NZ, n_group, SEATS, width), vm(*payload),
            vm(NZ, n_group, *tile, dtype=F32), vm(NZ, 8, rows, dtype=F32),
            vm(NZ, rows, rows, dtype=F32), vm(NZ, half, rows, dtype=F32),
            vm(NZ, rows, rows), vm(NZ, rows, rows),
            vm(*payload),
            vm(*payload), vm(*payload), vm(*payload),
            vm(CHUNKS, half_g, SEATS, width), vm(CHUNKS, half_g, SEATS, width),
            vm(*payload), vm(*payload), vm(*payload),
            vm(*payload), vm(*payload),
            vm(CHUNKS, 2, npairs, width), vm(CHUNKS, 2, npairs, width),
            dma((3,)),
            dma((2, CHUNKS)), dma((2, CHUNKS)), dma((4,)), dma((4,)),
            dma((CHUNKS, 6)), dma((CHUNKS, 6)), dma((NZ + 1,)), dma((NZ + 1,)),
            dma((CHUNKS, 6)), dma((CHUNKS, 6)), dma((2, CHUNKS)), dma((2, CHUNKS)),
            dma((2, CHUNKS)), dma((2, CHUNKS)), dma((2, CHUNKS)),
        ]
        return pl.pallas_call(
            functools.partial(second_kernel, seats),
            out_shape=(
                jax.ShapeDtypeStruct((npairs, width_d), BF16),
                jax.ShapeDtypeStruct((npairs, width_d), BF16),
            ),
            in_specs=[anywhere, anywhere, anywhere, in_vmem],
            out_specs=(anywhere, anywhere),
            scratch_shapes=scratch,
            compiler_params=pltpu.CompilerParams(
                collective_id=collective_id, has_side_effects=True, vmem_limit_bytes=67043328
            ),
        )

    return lax.cond(top[0, 0] <= FEW, rest(FEW, 1), rest(SEATS, 2), pay_p, pay_q, marks, unplace)


def solution(mesh):
    placed = (P(("grp", "dev"), None), P(("grp", "dev"), None), P(("grp", "dev"), None))
    return jax.shard_map(
        local,
        mesh=mesh,
        in_specs=placed,
        out_specs=(P(("grp", "dev"), None), P(("grp", "dev"), None)),
        check_vma=False,
    )
```

time: 390 us -> 164 us (0.42)
  Pallas kernels: 0 us -> 156 us
  blocking collectives: 136 us -> 0 us
  waiting for transfers between devices: 117 us -> 0 us
  local copies, waits for them, and re-layouts: 63.8 us -> 5.79 us
  matrix products: 45.7 us -> 0 us
  between operations: 14.1 us -> 1.31 us
  other arithmetic: 7.15 us -> 0 us
  starting transfers between devices: 5.22 us -> 0 us
    pallas_call x0 -> x2, Pallas kernels: none -> 156 us  [the longest x1 139 us: local(): lax.cond(top[0, 0] <= FEW, rest(FEW, 1), rest(SEATS, 2), pay_p, pay_q, ma...]
    all_to_all x2 -> x0, blocking collectives: 126 us -> none  [the longest x1 64.7 us: route_out(): lax.all_to_all(payload, ('grp', 'dev'), split_axis=0, concat_axis=0, tile...]
    reduce_scatter x1 -> x0, waiting for transfers between devices: 78.5 us -> none  [local(): lax.psum_scatter((inverse_temp * (block_term - own_rows)).astype(jnp.bflo...]
    dot_general x5 -> x0, matrix products: 45.7 us -> none  [the longest x1 16.6 us: local(): lax.dot_general(softmax_bf, q_here, (((0,), (0,)), ((), ())), preferred_e...]
    reshape x4 -> x0, local copies, waits for them, and re-layouts: 29.7 us -> none  [the longest x1 7.62 us: local(): jnp.concatenate([query_grad, passage_grad], axis=1)]
    all_gather x1 -> x0, waiting for transfers between devices: 29.4 us -> none  [local(): lax.all_gather(p_here, 'dev', axis=0, tiled=True)]
    gather x2 -> x0, local copies, waits for them, and re-layouts: 27.5 us -> none  [the longest x1 14.3 us: local(): own_rows = jnp.take(q_here, local_index, axis=0).astype(jnp.float32)]
    all_gather x1 -> x0, blocking collectives: 10.1 us -> none  [local(): lax.all_gather(slot_marks, 'dev', axis=0, tiled=True)]
  transfers between devices with their start and end apart: 3 -> 0, of which waited for: 3 -> 0; matrix products, arithmetic and copies ran while one was open for 10% -> 0% of each run, Pallas kernels for 0% -> 0%
where the time goes in v2:
time: 164 us; the launch traced here: 163 us
  Pallas kernels  156 us (95%)
  local copies, waits for them, and re-layouts  5.79 us (4%)
    pallas_call x1, Pallas kernels, local(): lax.cond(top[0, 0] <= FEW, rest(FEW, 1), rest(SEATS, 2), pay_p, pay_q, ma...  139 us
    pallas_call x1, Pallas kernels, local(): pl.pallas_call(first_kernel, out_shape=(jax.ShapeDtypeStruct(payload, BF1...  17.7 us
    unnamed x4, local copies, waits for them, and re-layouts  3.35 us

profile of v2, /device:TPU:1, one launch (start us, length us, event | category | flops | bytes accessed | tf_op | source)
XLA Modules:
  0.0 163.5 jit_solution(15447831425996161727)
XLA Ops:
  0.6 1.2 broadcast_in_dim.8.drow_ref
  1.9 17.7 %shard_map.54 = (bf16[8,16,32,256]{3,2,1,0:T(8,128)(2,1)}, bf16[8,16,32,256]{3,2,1,0:T(8,128)(2,1)}, f32[16,8,128]{2,1,0:T(8,128)}, bf16[256,512]{1,0:T(8,128)(2,1)}, f32[8,128]{1,0:T(8,128)}) custom-call(s32[8,128]{1,0:T(8,128)} %broadcast_in_dim.8.drow_ref, bf16[128,4096]{1,0:T(8,128)(2,1)} %q_ref.1, bf16[128,4096]{1,0:T(8,128)(2,1)} %p_ref.1), custom_call_target="tpu_custom_call" | custom-call | tf_op jit(solution)/shard_map/pallas_call | solution.py:497
  19.6 1.2 slice.3
  21.4 138.7 %conditional.1 = ((bf16[128,4096]{1,0:T(8,128)(2,1)}, bf16[128,4096]{1,0:T(8,128)(2,1)})) conditional(s32[]{:T(128)} %bitcast.1, (bf16[8,16,32,256]{3,2,1,0:T(8,128)(2,1)}, bf16[8,16,32,256]{3,2,1,0:T(8,128)(2,1)}, f32[16,8,128]{2,1,0:T(8,128)}, bf16[256,512]{1,0:T(8,128)(2,1)}) %tuple.13, (bf16[8,16,32,256]{3,2,1,0:T(8,128)(2,1)}, ...), branch_computations={%region_0.0_spmd, %region_1.0_spmd} | conditional | bytes 8 | solution.py:552
  21.6 138.5 %branch_1_fun.1 = (bf16[128,4096]{1,0:T(8,128)(2,1)}, bf16[128,4096]{1,0:T(8,128)(2,1)}) custom-call(bf16[8,16,32,256]{3,2,1,0:T(8,128)(2,1)} %get-tuple-element.20.pay_p, bf16[8,16,32,256]{3,2,1,0:T(8,128)(2,1)} %get-tuple-element.21.pay_q, f32[16,8,128]{2,1,0:T(8,128)} %get-tuple-element.22.marks_out, bf16[256,512]{1,0:T(8,128)(2,1)} %get-tuple-element.23.unplace), custom_call_target="tpu_custom_call" | custom-call | tf_op jit(solution)/shard_map/cond/branch_1_fun/pallas_call | solution.py:552
  160.1 0.0 copy-start
  160.1 2.4 %copy.15 = bf16[128,4096]{1,0:T(8,128)(2,1)} copy(bf16[128,4096]{1,0:T(8,128)(2,1)} %get-tuple-element.48) | data formatting | bytes 2097152
  162.5 0.0 copy-done
  162.5 1.0 copy.16
Async XLA Ops:
  160.1 2.4 %copy-start = (bf16[128,4096]{1,0:T(8,128)(2,1)S(1)}, bf16[128,4096]{1,0:T(8,128)(2,1)}, u32[]{:S(2)}) copy-start(bf16[128,4096]{1,0:T(8,128)(2,1)} %get-tuple-element.49) | copy-start | bytes 3145732

commit v3 on v2

--- a/solution.py
+++ b/solution.py
@@ -51,123 +51,14 @@
     return lambda: pl.semaphore_wait(barrier, n_group + 3)
 
 
-def first_kernel(
-    drow_ref, q_ref, p_ref, pay_p_ref, pay_q_ref, marks_ref, unplace_ref, top_ref,
-    dest, xp, xq, place, pay_p, pay_q, own_top, tops, plane_top, plane_tops,
-    swap_s, swap_r, local_s, keep_s, top_s, top_r, plane_s, plane_r,
-):
-    n_group = pay_p.shape[1]
-    npairs = q_ref.shape[0]
-    half_d = q_ref.shape[1] // 2
-    width = pay_p.shape[3]
-    rows = n_group * SEATS
-    g, d, c, up, down, far, mate = where_am_i()
-
-    mine = pl.ds(pl.multiple_of(c * half_d, half_d), half_d)
-    theirs = pl.ds(pl.multiple_of((1 - c) * half_d, half_d), half_d)
-    own_copies = [
-        pltpu.make_async_copy(drow_ref, dest.at[c], local_s.at[0]),
-        pltpu.make_async_copy(p_ref.at[:, mine], xp.at[c], local_s.at[1]),
-        pltpu.make_async_copy(q_ref.at[:, mine], xq.at[c], local_s.at[2]),
-    ]
-    for copy in own_copies:
-        copy.start()
-    greet(n_group)()
-    swaps = [
-        remote(drow_ref, dest.at[c], swap_s.at[0], swap_r.at[0], (g, mate)),
-        remote(p_ref.at[:, theirs], xp.at[c], swap_s.at[1], swap_r.at[1], (g, mate)),
-        remote(q_ref.at[:, theirs], xq.at[c], swap_s.at[2], swap_r.at[2], (g, mate)),
-    ]
-    for copy in swaps:
-        copy.start()
-
-    own_copies[0].wait()
-    swaps[0].wait_recv()
-    n2 = 2 * npairs
-    group = jnp.concatenate([dest[0, 0:1, :], dest[1, 0:1, :]], axis=1)
-    group = lax.shift_right_logical(group, jnp.full_like(group, 3))
-    count = jnp.sum(
-        jnp.where(lax.broadcasted_iota(jnp.int32, (n_group, n2), 0) == group, 1.0, 0.0), axis=1, keepdims=True
-    )
-    own_top[...] = jnp.broadcast_to(jnp.max(count, axis=0, keepdims=True), (8, 128))
-    tops[g] = own_top[...]
-
-    @pl.loop(1, n_group)
-    def _(o):
-        to = lax.rem(g + o, n_group)
-        remote(own_top, tops.at[g], top_s, top_r, (to, d)).start()
-
-    along = jnp.broadcast_to(group.astype(F32), (n2, n2))
-    across = along.T
-    i0 = lax.broadcasted_iota(jnp.int32, (n2, n2), 0)
-    i1 = lax.broadcasted_iota(jnp.int32, (n2, n2), 1)
-    same = along == across
-    rank_row = jnp.sum(jnp.where(same & (i0 < i1), 1.0, 0.0), axis=0, keepdims=True)
-    rank_col = jnp.sum(jnp.where(same & (i1 < i0), 1.0, 0.0), axis=1, keepdims=True)
-    slot_row = (group.astype(F32) * SEATS + rank_row).astype(jnp.int32)
-    slot_col = (across[:, 0:1] * SEATS + rank_col).astype(jnp.int32)
-    place[...] = jnp.where(
-        lax.broadcasted_iota(jnp.int32, (rows, n2), 0) == slot_row, 1.0, 0.0
-    ).astype(BF16)
-    unplace_ref[...] = jnp.where(
-        lax.broadcasted_iota(jnp.int32, (n2, rows), 1) == slot_col, 1.0, 0.0
-    ).astype(BF16)
-    lane = lax.broadcasted_iota(jnp.int32, (n_group, 128), 1) - lax.rem(g, 4) * SEATS
-    flags = jnp.where((lane >= 0) & (lane < count.astype(jnp.int32)), 1.0, 0.0)
-    for i in range(n_group):
-        marks_ref[i] = jnp.broadcast_to(flags[i : i + 1], (8, 128))
-
-    def fill(x, pay, pay_ref, which):
-        @pl.loop(0, CHUNKS)
-        def _(k):
-            cols = pl.ds(pl.multiple_of(k * width, width), width)
-            part = jnp.dot(place[...], x[:, :, cols].reshape(n2, width), preferred_element_type=F32)
-            pay[k] = part.astype(BF16).reshape(n_group, SEATS, width)
-            pltpu.make_async_copy(pay.at[k], pay_ref.at[k], keep_s.at[which, k]).start()
-
-    own_copies[1].wait()
-    swaps[1].wait_recv()
-    fill(xp, pay_p, pay_p_ref, 0)
-
-    wait_bytes(tops.at[pl.ds(0, n_group - 1)], top_r)
-    top = tops[0]
-    for i in range(1, n_group):
-        top = jnp.maximum(top, tops[i])
-    plane_top[...] = top
-    plane_copies = [
-        remote(plane_top, plane_tops.at[i], plane_s.at[i], plane_r.at[i], (g, to))
-        for i, to in enumerate((up, down, far))
-    ]
-    for copy in plane_copies:
-        copy.start()
-
-    own_copies[2].wait()
-    swaps[2].wait_recv()
-    fill(xq, pay_q, pay_q_ref, 1)
-
-    for copy in plane_copies:
-        copy.wait_recv()
-    top_ref[...] = jnp.maximum(
-        jnp.maximum(plane_top[...], plane_tops[0]), jnp.maximum(plane_tops[1], plane_tops[2])
-    )
-    for copy in swaps:
-        copy.wait_send()
-    for copy in plane_copies:
-        copy.wait_send()
-    wait_bytes(tops.at[pl.ds(0, n_group - 1)], top_s)
-
-    @pl.loop(0, CHUNKS)
-    def _(k):
-        pltpu.make_async_copy(pay_p.at[k], pay_p_ref.at[k], keep_s.at[0, k]).wait()
-        pltpu.make_async_copy(pay_q.at[k], pay_q_ref.at[k], keep_s.at[1, k]).wait()
-
-
-def second_kernel(
+def kernel(
     seats,
-    pay_p, pay_q, marks_out, unplace, oq_ref, op_ref,
+    drow_ref, q_ref, p_ref, oq_ref, op_ref, top_ref,
+    dest, xp, xq, place, unplace, pay_p, pay_q, marks_out, own_top, tops, plane_top, plane_tops,
     p_all, q_rows, marks, valid, scores, scores_in, soft, soft_t, dq, t1, t2, t3, ra, rb, rl, rr, dp,
     back_q, back_p, out_q, out_p,
-    local_s, place_s, place_r, mark_s, mark_r, ring_s, ring_r, core_s, core_r,
+    swap_s, swap_r, local_s, top_s, top_r, plane_s, plane_r,
+    place_s, place_r, mark_s, mark_r, ring_s, ring_r, core_s, core_r,
     sum_s, sum_r, back_s, back_r, keep_s, out_s, out_r,
 ):
     n_group = p_all.shape[2]
@@ -180,7 +71,28 @@
     g, d, c, up, down, far, mate = where_am_i()
     taken = pl.ds(0, seats)
 
+    first = pl.ds(pl.multiple_of(c * half_d, width), width)
+    others = pl.ds(pl.multiple_of(c * half_d + width, width), half_d - width)
+    mine = pl.ds(pl.multiple_of(c * half_d, half_d), half_d)
+    mate_first = pl.ds(pl.multiple_of((1 - c) * half_d, width), width)
+    mate_others = pl.ds(pl.multiple_of((1 - c) * half_d + width, width), half_d - width)
+    theirs = pl.ds(pl.multiple_of((1 - c) * half_d, half_d), half_d)
+    head, tail = pl.ds(0, width), pl.ds(width, half_d - width)
+    own_copies = [
+        pltpu.make_async_copy(drow_ref, dest.at[c], local_s.at[0]),
+        pltpu.make_async_copy(p_ref.at[:, first], xp.at[c, :, head], local_s.at[1]),
+        pltpu.make_async_copy(p_ref.at[:, others], xp.at[c, :, tail], local_s.at[2]),
+        pltpu.make_async_copy(q_ref.at[:, mine], xq.at[c], local_s.at[3]),
+    ]
+    swaps = [
+        remote(drow_ref, dest.at[c], swap_s.at[0], swap_r.at[0], (g, mate)),
+        remote(p_ref.at[:, mate_first], xp.at[c, :, head], swap_s.at[1], swap_r.at[1], (g, mate)),
+        remote(p_ref.at[:, mate_others], xp.at[c, :, tail], swap_s.at[2], swap_r.at[2], (g, mate)),
+        remote(q_ref.at[:, theirs], xq.at[c], swap_s.at[3], swap_r.at[3], (g, mate)),
+    ]
     ready = greet(n_group)
+    for copy in own_copies:
+        copy.start()
     if seats < SEATS:
         rest = slice(seats, SEATS)
         empty = jnp.zeros((n_group, SEATS - seats, width), BF16)
@@ -203,30 +115,72 @@
     def wait_all(ref, sem):
         wait_bytes(ref.at[pl.ds(0, n_group - 1), taken], sem)
 
-    def send_p(k):
-        send_all(pay_p.at[k], p_all.at[k, 0], place_s.at[0, k], place_r.at[0, k])
-
-    own_copies = [
-        pltpu.make_async_copy(pay_p.at[:, g, taken], p_all.at[:, 0, g, taken], local_s.at[0]),
-        pltpu.make_async_copy(pay_q.at[:, g, taken], q_rows.at[:, g, taken], local_s.at[1]),
-        pltpu.make_async_copy(marks_out.at[g], marks.at[0, g], local_s.at[2]),
-    ]
-    send_p(0)
-    for copy in own_copies:
+    for copy in swaps:
         copy.start()
+
+    def arrived(i):
+        own_copies[i].wait()
+        swaps[i].wait_recv()
+
+    arrived(0)
+    n2 = 2 * npairs
+    group = jnp.concatenate([dest[0, 0:1, :], dest[1, 0:1, :]], axis=1)
+    group = lax.shift_right_logical(group, jnp.full_like(group, 3))
+    along = jnp.broadcast_to(group.astype(F32), (n2, n2))
+    across = along.T
+    i0 = lax.broadcasted_iota(jnp.int32, (n2, n2), 0)
+    i1 = lax.broadcasted_iota(jnp.int32, (n2, n2), 1)
+    same = along == across
+    rank_row = jnp.sum(jnp.where(same & (i0 < i1), 1.0, 0.0), axis=0, keepdims=True)
+    slot_row = (group.astype(F32) * SEATS + rank_row).astype(jnp.int32)
+    place[...] = jnp.where(
+        lax.broadcasted_iota(jnp.int32, (rows, n2), 0) == slot_row, 1.0, 0.0
+    ).astype(BF16)
+
+    def fill(k, x, pay, into, which):
+        cols = pl.ds(k * width if isinstance(k, int) else pl.multiple_of(k * width, width), width)
+        part = jnp.dot(place[...], x[:, :, cols].reshape(n2, width), preferred_element_type=F32)
+        pay[k] = part.astype(BF16).reshape(n_group, SEATS, width)
+        send_all(pay.at[k], into, place_s.at[which, k], place_r.at[which, k])
+        into[g, 0:seats] = pay[k, g, 0:seats]
+
+    arrived(1)
+    fill(0, xp, pay_p, p_all.at[0, 0], 0)
+
+    count = jnp.sum(
+        jnp.where(lax.broadcasted_iota(jnp.int32, (n_group, n2), 0) == group, 1.0, 0.0), axis=1, keepdims=True
+    )
+    lane = lax.broadcasted_iota(jnp.int32, (n_group, 128), 1) - lax.rem(g, 4) * SEATS
+    flags = jnp.where((lane >= 0) & (lane < count.astype(jnp.int32)), 1.0, 0.0)
+    for i in range(n_group):
+        marks_out[i] = jnp.broadcast_to(flags[i : i + 1], (8, 128))
+    marks[0, g] = marks_out[g]
+    own_top[...] = jnp.broadcast_to(jnp.max(count, axis=0, keepdims=True), (8, 128))
+    tops[g] = own_top[...]
 
     @pl.loop(1, n_group)
     def _(o):
         to = lax.rem(g + o, n_group)
         remote(marks_out.at[to], marks.at[0, g], mark_s.at[0], mark_r.at[0], (to, d)).start()
+        remote(own_top, tops.at[g], top_s, top_r, (to, d)).start()
+
+    arrived(2)
 
     @pl.loop(1, CHUNKS)
     def _(k):
-        send_p(k)
+        fill(k, xp, pay_p, p_all.at[k, 0], 0)
+
+    arrived(3)
 
     @pl.loop(0, CHUNKS)
     def _(k):
-        send_all(pay_q.at[k], q_rows.at[k], place_s.at[1, k], place_r.at[1, k])
+        fill(k, xq, pay_q, q_rows.at[k], 1)
+
+    rank_col = jnp.sum(jnp.where(same & (i1 < i0), 1.0, 0.0), axis=1, keepdims=True)
+    slot_col = (across[:, 0:1] * SEATS + rank_col).astype(jnp.int32)
+    unplace[...] = jnp.where(
+        lax.broadcasted_iota(jnp.int32, (n2, rows), 1) == slot_col, 1.0, 0.0
+    ).astype(BF16)
 
     lo, hi = pl.ds(0, half_g), pl.ds(half_g, half_g)
 
@@ -274,8 +228,11 @@
         remote(marks.at[0], marks.at[2], mark_s.at[3], mark_r.at[3], (g, far)),
     ]
 
-    for copy in own_copies:
-        copy.wait()
+    plane_copies = [
+        remote(plane_top, plane_tops.at[i], plane_s.at[i], plane_r.at[i], (g, to))
+        for i, to in enumerate((up, down, far))
+    ]
+
     start_ring(0)
     wait_bytes(marks.at[0, pl.ds(0, n_group - 1)], mark_r.at[0])
     for copy in mark_ring:
@@ -294,6 +251,13 @@
             pieces.append(flag)
         flag = pieces[0] if len(pieces) == 1 else jnp.concatenate(pieces, axis=1)
         valid[j] = jnp.broadcast_to(flag[:, :rows], (8, rows))
+    wait_bytes(tops.at[pl.ds(0, n_group - 1)], top_r)
+    top = tops[0]
+    for i in range(1, n_group):
+        top = jnp.maximum(top, tops[i])
+    plane_top[...] = top
+    for copy in plane_copies:
+        copy.start()
     soft_t[0, :, 0:128] = jnp.broadcast_to(valid[0, 0:1, :], (128, rows)).T.astype(BF16)
 
     @pl.loop(2, CHUNKS)
@@ -302,6 +266,11 @@
         pass_on(step - 1)
         add_scores(step - 2)
 
+    for copy in plane_copies:
+        copy.wait_recv()
+    top_ref[...] = jnp.maximum(
+        jnp.maximum(plane_top[...], plane_tops[0]), jnp.maximum(plane_tops[1], plane_tops[2])
+    )
     pass_on(CHUNKS - 1)
     add_scores(CHUNKS - 2)
 
@@ -469,7 +438,8 @@
             there.wait()
 
     wait_bytes(marks_out.at[pl.ds(0, n_group - 1)], mark_s.at[0])
-    for copy in mark_ring:
+    wait_bytes(tops.at[pl.ds(0, n_group - 1)], top_s)
+    for copy in swaps + mark_ring + plane_copies:
         copy.wait_send()
     for j in range(NZ):
         share(j).wait_send()
@@ -494,31 +464,14 @@
 
     tile = (8, 128)
     payload = (CHUNKS, n_group, SEATS, width)
-    pay_p, pay_q, marks, unplace, top = pl.pallas_call(
-        first_kernel,
-        out_shape=(
-            jax.ShapeDtypeStruct(payload, BF16),
-            jax.ShapeDtypeStruct(payload, BF16),
-            jax.ShapeDtypeStruct((n_group, *tile), F32),
-            jax.ShapeDtypeStruct((2 * npairs, rows), BF16),
-            jax.ShapeDtypeStruct(tile, F32),
-        ),
-        in_specs=[in_vmem, anywhere, anywhere],
-        out_specs=(anywhere, anywhere, in_vmem, in_vmem, in_vmem),
-        scratch_shapes=[
+    def call(seats, collective_id):
+        scratch = [
             vm(2, 8, npairs, dtype=jnp.int32),
             vm(2, npairs, half_d), vm(2, npairs, half_d),
-            vm(rows, 2 * npairs),
-            vm(*payload), vm(*payload),
+            vm(rows, 2 * npairs), vm(2 * npairs, rows),
+            vm(*payload), vm(*payload), vm(n_group, *tile, dtype=F32),
             vm(*tile, dtype=F32), vm(n_group, *tile, dtype=F32),
             vm(*tile, dtype=F32), vm(3, *tile, dtype=F32),
-            dma((3,)), dma((3,)), dma((3,)), dma((2, CHUNKS)), dma(()), dma(()), dma((3,)), dma((3,)),
-        ],
-        compiler_params=pltpu.CompilerParams(collective_id=0, has_side_effects=True),
-    )(drow, queries, passages)
-
-    def rest(seats, collective_id):
-        scratch = [
             vm(CHUNKS, NZ, n_group, SEATS, width), vm(*payload),
             vm(NZ, n_group, *tile, dtype=F32), vm(NZ, 8, rows, dtype=F32),
             vm(NZ, rows, rows, dtype=F32), vm(NZ, half, rows, dtype=F32),
@@ -529,27 +482,31 @@
             vm(*payload), vm(*payload), vm(*payload),
             vm(*payload), vm(*payload),
             vm(CHUNKS, 2, npairs, width), vm(CHUNKS, 2, npairs, width),
-            dma((3,)),
+            dma((4,)), dma((4,)), dma((4,)), dma(()), dma(()), dma((3,)), dma((3,)),
             dma((2, CHUNKS)), dma((2, CHUNKS)), dma((4,)), dma((4,)),
             dma((CHUNKS, 6)), dma((CHUNKS, 6)), dma((NZ + 1,)), dma((NZ + 1,)),
             dma((CHUNKS, 6)), dma((CHUNKS, 6)), dma((2, CHUNKS)), dma((2, CHUNKS)),
             dma((2, CHUNKS)), dma((2, CHUNKS)), dma((2, CHUNKS)),
         ]
         return pl.pallas_call(
-            functools.partial(second_kernel, seats),
+            functools.partial(kernel, seats),
             out_shape=(
                 jax.ShapeDtypeStruct((npairs, width_d), BF16),
                 jax.ShapeDtypeStruct((npairs, width_d), BF16),
+                jax.ShapeDtypeStruct(tile, F32),
             ),
-            in_specs=[anywhere, anywhere, anywhere, in_vmem],
-            out_specs=(anywhere, anywhere),
+            in_specs=[in_vmem, anywhere, anywhere],
+            out_specs=(anywhere, anywhere, in_vmem),
             scratch_shapes=scratch,
             compiler_params=pltpu.CompilerParams(
                 collective_id=collective_id, has_side_effects=True, vmem_limit_bytes=67043328
             ),
-        )
-
-    return lax.cond(top[0, 0] <= FEW, rest(FEW, 1), rest(SEATS, 2), pay_p, pay_q, marks, unplace)
+        )(drow, queries, passages)
+
+    query_grads, passage_grads, top = call(FEW, 0)
+    return lax.cond(
+        top[0, 0] <= FEW, lambda: (query_grads, passage_grads), lambda: tuple(call(SEATS, 1)[:2])
+    )
 
 
 def solution(mesh):

time: 164 us -> 156 us (0.951)
  Pallas kernels: 156 us -> 148 us
    pallas_call x2 -> x1, Pallas kernels: 156 us -> 148 us  [call(): pl.pallas_call(functools.partial(kernel, seats), out_shape=(jax.ShapeDtyp...]
    unnamed x4 -> x6, local copies, waits for them, and re-layouts: 3.35 us -> 4 us
where the time goes in v3:
time: 156 us; the launch traced here: 155 us
  Pallas kernels  148 us (95%)
  local copies, waits for them, and re-layouts  5.77 us (4%)
    pallas_call x1, Pallas kernels, call(): pl.pallas_call(functools.partial(kernel, seats), out_shape=(jax.ShapeDtyp...  148 us
    unnamed x6, local copies, waits for them, and re-layouts  4 us

profile of v3, /device:TPU:1, one launch (start us, length us, event | category | flops | bytes accessed | tf_op | source)
XLA Modules:
  0.0 155.4 jit_solution(14368605526050880159)
XLA Ops:
  0.6 0.0 copy-start.1
  0.6 0.6 copy-done.1
  1.3 0.6 broadcast_in_dim.8.drow_ref
  1.9 148.1 %shard_map.50 = (bf16[128,4096]{1,0:T(8,128)(2,1)}, bf16[128,4096]{1,0:T(8,128)(2,1)}, f32[8,128]{1,0:T(8,128)}) custom-call(s32[8,128]{1,0:T(8,128)} %broadcast_in_dim.8.drow_ref, bf16[128,4096]{1,0:T(8,128)(2,1)} %q_ref.1, bf16[128,4096]{1,0:T(8,128)(2,1)} %p_ref.1), custom_call_target="tpu_custom_call" | custom-call | tf_op jit(solution)/shard_map/pallas_call | solution.py:491
  150.0 1.2 slice.3
  151.8 0.2 conditional.1
  152.0 0.0 copy-start
  152.0 2.4 %copy.11 = bf16[128,4096]{1,0:T(8,128)(2,1)} copy(bf16[128,4096]{1,0:T(8,128)(2,1)} %get-tuple-element.29) | data formatting | bytes 2097152
  154.4 0.0 copy-done
  154.4 1.0 copy.12
Async XLA Ops:
  0.6 0.7 copy-start.1
  152.0 2.4 %copy-start = (bf16[128,4096]{1,0:T(8,128)(2,1)S(1)}, bf16[128,4096]{1,0:T(8,128)(2,1)}, u32[]{:S(2)}) copy-start(bf16[128,4096]{1,0:T(8,128)(2,1)} %get-tuple-element.30) | copy-start | bytes 3145732

commit v4 on v3

--- a/solution.py
+++ b/solution.py
@@ -58,7 +58,7 @@
     p_all, q_rows, marks, valid, scores, scores_in, soft, soft_t, dq, t1, t2, t3, ra, rb, rl, rr, dp,
     back_q, back_p, out_q, out_p,
     swap_s, swap_r, local_s, top_s, top_r, plane_s, plane_r,
-    place_s, place_r, mark_s, mark_r, ring_s, ring_r, core_s, core_r,
+    place_s, place_r, mark_s, mark_r, ring_s, ring_r, core_s, core_r, give_s, give_r,
     sum_s, sum_r, back_s, back_r, keep_s, out_s, out_r,
 ):
     n_group = p_all.shape[2]
@@ -166,21 +166,13 @@
 
     arrived(2)
 
-    @pl.loop(1, CHUNKS)
-    def _(k):
+    def fill_p(k):
         fill(k, xp, pay_p, p_all.at[k, 0], 0)
 
-    arrived(3)
-
-    @pl.loop(0, CHUNKS)
-    def _(k):
+    def fill_q(k):
         fill(k, xq, pay_q, q_rows.at[k], 1)
 
-    rank_col = jnp.sum(jnp.where(same & (i1 < i0), 1.0, 0.0), axis=1, keepdims=True)
-    slot_col = (across[:, 0:1] * SEATS + rank_col).astype(jnp.int32)
-    unplace[...] = jnp.where(
-        lax.broadcasted_iota(jnp.int32, (n2, rows), 1) == slot_col, 1.0, 0.0
-    ).astype(BF16)
+    fill_p(1)
 
     lo, hi = pl.ds(0, half_g), pl.ds(half_g, half_g)
 
@@ -200,7 +192,7 @@
         return lax.dot_general(
             q_rows[k].reshape(rows, width), p_all[k, j].reshape(rows, width),
             (((1,), (1,)), ((), ())), preferred_element_type=F32,
-        )
+        ).reshape(n_group, SEATS, rows)
 
     def start_ring(k):
         wait_all(p_all.at[k, 0], place_r.at[0, k])
@@ -234,12 +226,23 @@
     ]
 
     start_ring(0)
+    fill_p(2)
+    arrived(3)
+    fill_q(0)
     wait_bytes(marks.at[0, pl.ds(0, n_group - 1)], mark_r.at[0])
     for copy in mark_ring:
         copy.start()
     start_ring(1)
     pass_on(0)
+    fill_p(3)
+    fill_q(1)
     scores[...] = jnp.zeros_like(scores)
+    soft[...] = jnp.zeros_like(soft)
+    rank_col = jnp.sum(jnp.where(same & (i1 < i0), 1.0, 0.0), axis=1, keepdims=True)
+    slot_col = (across[:, 0:1] * SEATS + rank_col).astype(jnp.int32)
+    unplace[...] = jnp.where(
+        lax.broadcasted_iota(jnp.int32, (n2, rows), 1) == slot_col, 1.0, 0.0
+    ).astype(BF16)
     for copy in mark_ring:
         copy.wait_recv()
     for j in range(NZ):
@@ -260,10 +263,19 @@
         copy.start()
     soft_t[0, :, 0:128] = jnp.broadcast_to(valid[0, 0:1, :], (128, rows)).T.astype(BF16)
 
-    @pl.loop(2, CHUNKS)
+    @pl.loop(2, CHUNKS - 2)
     def _(step):
         start_ring(step)
         pass_on(step - 1)
+        fill_p(step + 2)
+        fill_q(step)
+        add_scores(step - 2)
+
+    @pl.loop(CHUNKS - 2, CHUNKS)
+    def _(step):
+        start_ring(step)
+        pass_on(step - 1)
+        fill_q(step)
         add_scores(step - 2)
 
     for copy in plane_copies:
@@ -274,11 +286,10 @@
     pass_on(CHUNKS - 1)
     add_scores(CHUNKS - 2)
 
-    my_rows = pl.ds(pl.multiple_of(c * half, half), half)
-    mate_rows = pl.ds(pl.multiple_of((1 - c) * half, half), half)
+    mate_seats = pl.ds((1 - c) * half_g, half_g)
 
     def share(j):
-        return remote(scores.at[j, mate_rows], scores_in.at[j], core_s.at[j], core_r.at[j], (g, mate))
+        return remote(scores.at[j, mate_seats, taken], scores_in.at[j, :, taken], core_s.at[j], core_r.at[j], (g, mate))
 
     last = CHUNKS - 1
     wait_all(q_rows.at[last], place_r.at[1, last])
@@ -290,17 +301,13 @@
     for j in range(NZ):
         share(j).wait_recv()
 
-    tile = min(16, half)
-
-    @pl.loop(0, half // tile)
-    def _(i):
-        at_out = pl.ds(pl.multiple_of(c * half + i * tile, tile), tile)
-        at_in = pl.ds(pl.multiple_of(i * tile, tile), tile)
-        keep = soft_t[0, at_out, 0:1].astype(F32)
+    def softmax_of(i):
+        n = c * half_g + i
+        keep = soft_t[0, pl.ds(pl.multiple_of(n * SEATS, SEATS), SEATS), 0:1].astype(F32)
         parts = []
         top = None
         for j in range(NZ):
-            s = inverse_temp * (scores[j, at_out, :] + scores_in[j, at_in, :])
+            s = inverse_temp * (scores[j, n] + scores_in[j, i])
             s = jnp.where(valid[j, 0:1, :] > 0, s, -1e30)
             parts.append(s)
             m = jnp.max(s, axis=1, keepdims=True)
@@ -313,22 +320,36 @@
             t = jnp.sum(e, axis=1, keepdims=True)
             total = t if total is None else total + t
         for j in range(NZ):
-            soft[j, at_out, :] = (exps[j] / total * keep).astype(BF16)
-
-    give = remote(soft.at[:, my_rows], soft.at[:, my_rows], core_s.at[NZ], core_r.at[NZ], (g, mate))
-    give.start()
+            soft[j, n] = jnp.where(keep > 0, exps[j] / total, 0.0).astype(BF16)
+
+    pieces = min(4, half_g)
+    piece = half_g // pieces
+
+    def give(i):
+        part = pl.ds(c * half_g + i * piece, piece)
+        return remote(soft.at[:, part, taken], soft.at[:, part, taken], give_s.at[i], give_r.at[i], (g, mate))
+
+    for i in range(pieces):
+
+        @pl.loop(i * piece, (i + 1) * piece, unroll=True)
+        def _(n):
+            softmax_of(n)
+
+        give(i).start()
     my_lanes = pl.ds(pl.multiple_of(c * half, half), half)
     mate_lanes = pl.ds(pl.multiple_of((1 - c) * half, half), half)
+    my_seats = pl.ds(c * half_g, half_g)
 
     @pl.loop(0, NZ)
     def _(j):
-        soft_t[j, :, my_lanes] = soft[j, my_rows, :].T
-
-    give.wait_recv()
+        soft_t[j, :, my_lanes] = soft[j, my_seats].reshape(half, rows).T
+
+    for i in range(pieces):
+        give(i).wait_recv()
 
     @pl.loop(0, NZ)
     def _(j):
-        soft_t[j, :, mate_lanes] = soft[j, mate_rows, :].T
+        soft_t[j, :, mate_lanes] = soft[j, mate_seats].reshape(half, rows).T
 
     def q_of(k):
         return q_rows[k].reshape(rows, width)
@@ -370,7 +391,7 @@
     def query_part(k):
         acc = -p_all[k, 0].reshape(rows, width).astype(F32)
         for j in range(NZ):
-            acc = acc + jnp.dot(soft[j], p_all[k, j].reshape(rows, width), preferred_element_type=F32)
+            acc = acc + jnp.dot(soft[j].reshape(rows, rows), p_all[k, j].reshape(rows, width), preferred_element_type=F32)
         dq[k] = blocks(inverse_temp * acc)
         send_all(dq.at[k], back_q.at[k], back_s.at[0, k], back_r.at[0, k])
         back_q[k, g, 0:seats] = dq[k, g, 0:seats]
@@ -443,7 +464,8 @@
         copy.wait_send()
     for j in range(NZ):
         share(j).wait_send()
-    give.wait_send()
+    for i in range(pieces):
+        give(i).wait_send()
 
 
 def local(queries, passages, destination):
@@ -474,8 +496,8 @@
             vm(*tile, dtype=F32), vm(3, *tile, dtype=F32),
             vm(CHUNKS, NZ, n_group, SEATS, width), vm(*payload),
             vm(NZ, n_group, *tile, dtype=F32), vm(NZ, 8, rows, dtype=F32),
-            vm(NZ, rows, rows, dtype=F32), vm(NZ, half, rows, dtype=F32),
-            vm(NZ, rows, rows), vm(NZ, rows, rows),
+            vm(NZ, n_group, SEATS, rows, dtype=F32), vm(NZ, half_g, SEATS, rows, dtype=F32),
+            vm(NZ, n_group, SEATS, rows), vm(NZ, rows, rows),
             vm(*payload),
             vm(*payload), vm(*payload), vm(*payload),
             vm(CHUNKS, half_g, SEATS, width), vm(CHUNKS, half_g, SEATS, width),
@@ -484,7 +506,7 @@
             vm(CHUNKS, 2, npairs, width), vm(CHUNKS, 2, npairs, width),
             dma((4,)), dma((4,)), dma((4,)), dma(()), dma(()), dma((3,)), dma((3,)),
             dma((2, CHUNKS)), dma((2, CHUNKS)), dma((4,)), dma((4,)),
-            dma((CHUNKS, 6)), dma((CHUNKS, 6)), dma((NZ + 1,)), dma((NZ + 1,)),
+            dma((CHUNKS, 6)), dma((CHUNKS, 6)), dma((NZ,)), dma((NZ,)), dma((4,)), dma((4,)),
             dma((CHUNKS, 6)), dma((CHUNKS, 6)), dma((2, CHUNKS)), dma((2, CHUNKS)),
             dma((2, CHUNKS)), dma((2, CHUNKS)), dma((2, CHUNKS)),
         ]

time: 156 us -> 150 us (0.962)
  Pallas kernels: 148 us -> 142 us
    pallas_call x1, Pallas kernels: 148 us -> 142 us  [call(): pl.pallas_call(functools.partial(kernel, seats), out_shape=(jax.ShapeDtyp...]
where the time goes in v4:
time: 150 us
  Pallas kernels  142 us (95%)
  local copies, waits for them, and re-layouts  5.77 us (4%)
    pallas_call x1, Pallas kernels, call(): pl.pallas_call(functools.partial(kernel, seats), out_shape=(jax.ShapeDtyp...  142 us
    unnamed x6, local copies, waits for them, and re-layouts  4 us

profile of v4, /device:TPU:1, one launch (start us, length us, event | category | flops | bytes accessed | tf_op | source)
XLA Modules:
  0.0 149.5 jit_solution(12031996840486345517)
XLA Ops:
  0.6 0.0 copy-start.1
  0.6 0.6 copy-done.1
  1.3 0.6 broadcast_in_dim.8.drow_ref
  1.9 142.2 %shard_map.50 = (bf16[128,4096]{1,0:T(8,128)(2,1)}, bf16[128,4096]{1,0:T(8,128)(2,1)}, f32[8,128]{1,0:T(8,128)}) custom-call(s32[8,128]{1,0:T(8,128)} %broadcast_in_dim.8.drow_ref, bf16[128,4096]{1,0:T(8,128)(2,1)} %q_ref.1, bf16[128,4096]{1,0:T(8,128)(2,1)} %p_ref.1), custom_call_target="tpu_custom_call" | custom-call | tf_op jit(solution)/shard_map/pallas_call | solution.py:513
  144.1 1.2 slice.3
  145.9 0.2 conditional.1
  146.1 0.0 copy-start
  146.2 2.4 %copy.11 = bf16[128,4096]{1,0:T(8,128)(2,1)} copy(bf16[128,4096]{1,0:T(8,128)(2,1)} %get-tuple-element.29) | data formatting | bytes 2097152
  148.5 0.0 copy-done
  148.5 1.0 copy.12
Async XLA Ops:
  0.6 0.7 copy-start.1
  146.1 2.4 %copy-start = (bf16[128,4096]{1,0:T(8,128)(2,1)S(1)}, bf16[128,4096]{1,0:T(8,128)(2,1)}, u32[]{:S(2)}) copy-start(bf16[128,4096]{1,0:T(8,128)(2,1)} %get-tuple-element.30) | copy-start | bytes 3145732

commit v5 on v4

--- a/solution.py
+++ b/solution.py
@@ -13,6 +13,7 @@
 FEW = 24
 NZ = 4
 CHUNKS = 8
+RAW = 2
 F32, BF16 = jnp.float32, jnp.bfloat16
 
 
@@ -54,10 +55,10 @@
 def kernel(
     seats,
     drow_ref, q_ref, p_ref, oq_ref, op_ref, top_ref,
-    dest, xp, xq, place, unplace, pay_p, pay_q, marks_out, own_top, tops, plane_top, plane_tops,
+    dest, raw_x, raw_pay, xp, xq, place, unplace, pay_p, pay_q, marks_out, own_top, tops, plane_top, plane_tops,
     p_all, q_rows, marks, valid, scores, scores_in, soft, soft_t, dq, t1, t2, t3, ra, rb, rl, rr, dp,
     back_q, back_p, out_q, out_p,
-    swap_s, swap_r, local_s, top_s, top_r, plane_s, plane_r,
+    swap_s, swap_r, local_s, dest_s, dest_r, raw_s, raw_r, top_s, top_r, plane_s, plane_r,
     place_s, place_r, mark_s, mark_r, ring_s, ring_r, core_s, core_r, give_s, give_r,
     sum_s, sum_r, back_s, back_r, keep_s, out_s, out_r,
 ):
@@ -71,22 +72,23 @@
     g, d, c, up, down, far, mate = where_am_i()
     taken = pl.ds(0, seats)
 
-    first = pl.ds(pl.multiple_of(c * half_d, width), width)
-    others = pl.ds(pl.multiple_of(c * half_d + width, width), half_d - width)
+    early = RAW * width
+    first = pl.ds(pl.multiple_of(c * half_d, early), early)
+    others = pl.ds(pl.multiple_of(c * half_d + early, early), half_d - early)
     mine = pl.ds(pl.multiple_of(c * half_d, half_d), half_d)
-    mate_first = pl.ds(pl.multiple_of((1 - c) * half_d, width), width)
-    mate_others = pl.ds(pl.multiple_of((1 - c) * half_d + width, width), half_d - width)
+    mate_first = pl.ds(pl.multiple_of((1 - c) * half_d, early), early)
+    mate_others = pl.ds(pl.multiple_of((1 - c) * half_d + early, early), half_d - early)
     theirs = pl.ds(pl.multiple_of((1 - c) * half_d, half_d), half_d)
-    head, tail = pl.ds(0, width), pl.ds(width, half_d - width)
+    tail = pl.ds(early, half_d - early)
     own_copies = [
-        pltpu.make_async_copy(drow_ref, dest.at[c], local_s.at[0]),
-        pltpu.make_async_copy(p_ref.at[:, first], xp.at[c, :, head], local_s.at[1]),
+        pltpu.make_async_copy(drow_ref, dest.at[0, c], local_s.at[0]),
+        pltpu.make_async_copy(p_ref.at[:, first], raw_x.at[0, c], local_s.at[1]),
         pltpu.make_async_copy(p_ref.at[:, others], xp.at[c, :, tail], local_s.at[2]),
         pltpu.make_async_copy(q_ref.at[:, mine], xq.at[c], local_s.at[3]),
     ]
     swaps = [
-        remote(drow_ref, dest.at[c], swap_s.at[0], swap_r.at[0], (g, mate)),
-        remote(p_ref.at[:, mate_first], xp.at[c, :, head], swap_s.at[1], swap_r.at[1], (g, mate)),
+        remote(drow_ref, dest.at[0, c], swap_s.at[0], swap_r.at[0], (g, mate)),
+        remote(p_ref.at[:, mate_first], raw_x.at[0, c], swap_s.at[1], swap_r.at[1], (g, mate)),
         remote(p_ref.at[:, mate_others], xp.at[c, :, tail], swap_s.at[2], swap_r.at[2], (g, mate)),
         remote(q_ref.at[:, theirs], xq.at[c], swap_s.at[3], swap_r.at[3], (g, mate)),
     ]
@@ -122,30 +124,82 @@
         own_copies[i].wait()
         swaps[i].wait_recv()
 
-    arrived(0)
     n2 = 2 * npairs
-    group = jnp.concatenate([dest[0, 0:1, :], dest[1, 0:1, :]], axis=1)
-    group = lax.shift_right_logical(group, jnp.full_like(group, 3))
-    along = jnp.broadcast_to(group.astype(F32), (n2, n2))
-    across = along.T
     i0 = lax.broadcasted_iota(jnp.int32, (n2, n2), 0)
     i1 = lax.broadcasted_iota(jnp.int32, (n2, n2), 1)
-    same = along == across
-    rank_row = jnp.sum(jnp.where(same & (i0 < i1), 1.0, 0.0), axis=0, keepdims=True)
-    slot_row = (group.astype(F32) * SEATS + rank_row).astype(jnp.int32)
-    place[...] = jnp.where(
-        lax.broadcasted_iota(jnp.int32, (rows, n2), 0) == slot_row, 1.0, 0.0
-    ).astype(BF16)
-
-    def fill(k, x, pay, into, which):
-        cols = pl.ds(k * width if isinstance(k, int) else pl.multiple_of(k * width, width), width)
-        part = jnp.dot(place[...], x[:, :, cols].reshape(n2, width), preferred_element_type=F32)
-        pay[k] = part.astype(BF16).reshape(n_group, SEATS, width)
-        send_all(pay.at[k], into, place_s.at[which, k], place_r.at[which, k])
-        into[g, 0:seats] = pay[k, g, 0:seats]
-
+
+    def groups_of(j):
+        group = jnp.concatenate([dest[j, 0, 0:1, :], dest[j, 1, 0:1, :]], axis=1)
+        group = lax.shift_right_logical(group, jnp.full_like(group, 3))
+        across = jnp.broadcast_to(group.astype(F32), (n2, n2)).T
+        return group, across, group.astype(F32) == across
+
+    def placing(group, same):
+        rank_row = jnp.sum(jnp.where(same & (i0 < i1), 1.0, 0.0), axis=0, keepdims=True)
+        slot_row = (group.astype(F32) * SEATS + rank_row).astype(jnp.int32)
+        return jnp.where(lax.broadcasted_iota(jnp.int32, (rows, n2), 0) == slot_row, 1.0, 0.0).astype(BF16)
+
+    dest_copies = [
+        remote(dest.at[0], dest.at[j], dest_s.at[j - 1], dest_r.at[j - 1], (g, to))
+        for j, to in ((1, down), (2, far), (3, up))
+    ]
+
+    def raw(i):
+        src, dst, core, to = (
+            (0, 3, 0, up), (0, 3, 1, up), (0, 1, 1, down), (0, 1, 0, down), (3, 2, 0, up), (1, 2, 1, down)
+        )[i]
+        return remote(raw_x.at[src, core], raw_x.at[dst, core], ring_s.at[0, i], ring_r.at[0, i], (g, to))
+
+    arrived(0)
     arrived(1)
-    fill(0, xp, pay_p, p_all.at[0, 0], 0)
+    for i in (0, 2, 1, 3):
+        raw(i).start()
+    for copy in dest_copies:
+        copy.start()
+    group, across, same = groups_of(0)
+    place[...] = placing(group, same)
+
+    def fill_from(placer, x, pay, into, s, r):
+        part = jnp.dot(placer, x.reshape(n2, width), preferred_element_type=F32)
+        pay[...] = part.astype(BF16).reshape(n_group, SEATS, width)
+        send_all(pay, into, s, r)
+        into[g, 0:seats] = pay[g, 0:seats]
+
+    def columns(k):
+        return pl.ds(k * width if isinstance(k, int) else pl.multiple_of(k * width, width), width)
+
+    def fill_p(k):
+        fill_from(
+            place[...], xp[:, :, columns(k)], pay_p.at[k], p_all.at[k, 0], place_s.at[0, k], place_r.at[0, k]
+        )
+
+    def fill_q(k):
+        fill_from(place[...], xq[:, :, columns(k)], pay_q.at[k], q_rows.at[k], place_s.at[1, k], place_r.at[1, k])
+
+    def fill_own(k):
+        fill_from(
+            place[...], raw_x[0, :, :, columns(k)], pay_p.at[k], p_all.at[k, 0], place_s.at[0, k], place_r.at[0, k]
+        )
+
+    def fill_raw(j):
+        group, _, same = groups_of(j)
+        placer = placing(group, same)
+        for k in range(RAW):
+            fill_from(
+                placer, raw_x[j, :, :, columns(k)], raw_pay.at[k, j - 1], p_all.at[k, j],
+                raw_s.at[k, j - 1], raw_r.at[k, j - 1],
+            )
+
+    arrived(2)
+    fill_p(2)
+    raw(0).wait_recv()
+    raw(4).start()
+    raw(2).wait_recv()
+    raw(5).start()
+
+    @pl.loop(3, 5)
+    def _(k):
+        fill_p(k)
 
     count = jnp.sum(
         jnp.where(lax.broadcasted_iota(jnp.int32, (n_group, n2), 0) == group, 1.0, 0.0), axis=1, keepdims=True
@@ -164,15 +218,8 @@
         remote(marks_out.at[to], marks.at[0, g], mark_s.at[0], mark_r.at[0], (to, d)).start()
         remote(own_top, tops.at[g], top_s, top_r, (to, d)).start()
 
-    arrived(2)
-
-    def fill_p(k):
-        fill(k, xp, pay_p, p_all.at[k, 0], 0)
-
-    def fill_q(k):
-        fill(k, xq, pay_q, q_rows.at[k], 1)
-
-    fill_p(1)
+    arrived(3)
+    fill_q(2)
 
     lo, hi = pl.ds(0, half_g), pl.ds(half_g, half_g)
 
@@ -207,8 +254,13 @@
 
     def add_scores(k):
         wait_all(q_rows.at[k], place_r.at[1, k])
-        for i in (1, 3, 4, 5):
-            ring(k, i).wait_recv()
+        if isinstance(k, int) and k < RAW:
+            wait_all(p_all.at[k, 0], place_r.at[0, k])
+            for j in range(1, NZ):
+                wait_all(p_all.at[k, j], raw_r.at[k, j - 1])
+        else:
+            for i in (1, 3, 4, 5):
+                ring(k, i).wait_recv()
 
         @pl.loop(0, NZ)
         def _(j):
@@ -225,17 +277,13 @@
         for i, to in enumerate((up, down, far))
     ]
 
-    start_ring(0)
-    fill_p(2)
-    arrived(3)
-    fill_q(0)
+    start_ring(2)
+    fill_p(5)
+    fill_q(3)
+    fill_p(6)
     wait_bytes(marks.at[0, pl.ds(0, n_group - 1)], mark_r.at[0])
     for copy in mark_ring:
         copy.start()
-    start_ring(1)
-    pass_on(0)
-    fill_p(3)
-    fill_q(1)
     scores[...] = jnp.zeros_like(scores)
     soft[...] = jnp.zeros_like(soft)
     rank_col = jnp.sum(jnp.where(same & (i1 < i0), 1.0, 0.0), axis=1, keepdims=True)
@@ -243,13 +291,18 @@
     unplace[...] = jnp.where(
         lax.broadcasted_iota(jnp.int32, (n2, rows), 1) == slot_col, 1.0, 0.0
     ).astype(BF16)
+
+    start_ring(3)
+    pass_on(2)
+    fill_p(7)
+    fill_q(4)
     for copy in mark_ring:
         copy.wait_recv()
     for j in range(NZ):
         pieces = []
-        for first in range(0, n_group, 4):
-            flag = marks[j, first, 0:1, :]
-            for i in range(first + 1, min(first + 4, n_group)):
+        for first_mark in range(0, n_group, 4):
+            flag = marks[j, first_mark, 0:1, :]
+            for i in range(first_mark + 1, min(first_mark + 4, n_group)):
                 flag = flag + marks[j, i, 0:1, :]
             pieces.append(flag)
         flag = pieces[0] if len(pieces) == 1 else jnp.concatenate(pieces, axis=1)
@@ -262,29 +315,36 @@
     for copy in plane_copies:
         copy.start()
     soft_t[0, :, 0:128] = jnp.broadcast_to(valid[0, 0:1, :], (128, rows)).T.astype(BF16)
-
-    @pl.loop(2, CHUNKS - 2)
+    for copy in dest_copies:
+        copy.wait_recv()
+    for i in (1, 3, 4, 5):
+        raw(i).wait_recv()
+
+    for k in range(RAW):
+        fill_own(k)
+
+    @pl.loop(4, 7)
     def _(step):
         start_ring(step)
         pass_on(step - 1)
-        fill_p(step + 2)
-        fill_q(step)
+        fill_raw(step - 3)
+        fill_q(step + 1)
         add_scores(step - 2)
 
-    @pl.loop(CHUNKS - 2, CHUNKS)
-    def _(step):
-        start_ring(step)
-        pass_on(step - 1)
-        fill_q(step)
-        add_scores(step - 2)
-
+    start_ring(7)
+    pass_on(6)
+    fill_q(0)
+    fill_q(1)
+    add_scores(5)
     for copy in plane_copies:
         copy.wait_recv()
     top_ref[...] = jnp.maximum(
         jnp.maximum(plane_top[...], plane_tops[0]), jnp.maximum(plane_tops[1], plane_tops[2])
     )
-    pass_on(CHUNKS - 1)
-    add_scores(CHUNKS - 2)
+    pass_on(7)
+    add_scores(6)
+    add_scores(0)
+    add_scores(1)
 
     mate_seats = pl.ds((1 - c) * half_g, half_g)
 
@@ -451,7 +511,6 @@
         wait_all(dq.at[k], back_s.at[0, k])
         wait_all(dp.at[k], back_s.at[1, k])
         for i in range(6):
-            ring(k, i).wait_send()
             summed(k, i).wait_send()
         for which in range(2):
             here, there = outputs(k, which)
@@ -459,8 +518,18 @@
             there.wait()
 
     wait_bytes(marks_out.at[pl.ds(0, n_group - 1)], mark_s.at[0])
+    @pl.loop(RAW, CHUNKS)
+    def _(k):
+        for i in range(6):
+            ring(k, i).wait_send()
+
+    for i in range(6):
+        raw(i).wait_send()
+    for k in range(RAW):
+        for j in range(NZ - 1):
+            wait_all(raw_pay.at[k, j], raw_s.at[k, j])
     wait_bytes(tops.at[pl.ds(0, n_group - 1)], top_s)
-    for copy in swaps + mark_ring + plane_copies:
+    for copy in swaps + dest_copies + mark_ring + plane_copies:
         copy.wait_send()
     for j in range(NZ):
         share(j).wait_send()
@@ -488,7 +557,8 @@
     payload = (CHUNKS, n_group, SEATS, width)
     def call(seats, collective_id):
         scratch = [
-            vm(2, 8, npairs, dtype=jnp.int32),
+            vm(NZ, 2, 8, npairs, dtype=jnp.int32),
+            vm(NZ, 2, npairs, RAW * width), vm(RAW, NZ - 1, n_group, SEATS, width),
             vm(2, npairs, half_d), vm(2, npairs, half_d),
             vm(rows, 2 * npairs), vm(2 * npairs, rows),
             vm(*payload), vm(*payload), vm(n_group, *tile, dtype=F32),
@@ -504,7 +574,8 @@
             vm(*payload), vm(*payload), vm(*payload),
             vm(*payload), vm(*payload),
             vm(CHUNKS, 2, npairs, width), vm(CHUNKS, 2, npairs, width),
-            dma((4,)), dma((4,)), dma((4,)), dma(()), dma(()), dma((3,)), dma((3,)),
+            dma((4,)), dma((4,)), dma((4,)), dma((3,)), dma((3,)), dma((RAW, 3)), dma((RAW, 3)),
+            dma(()), dma(()), dma((3,)), dma((3,)),
             dma((2, CHUNKS)), dma((2, CHUNKS)), dma((4,)), dma((4,)),
             dma((CHUNKS, 6)), dma((CHUNKS, 6)), dma((NZ,)), dma((NZ,)), dma((4,)), dma((4,)),
             dma((CHUNKS, 6)), dma((CHUNKS, 6)), dma((2, CHUNKS)), dma((2, CHUNKS)),

time: 150 us -> 146 us (0.973)
  Pallas kernels: 142 us -> 139 us
    pallas_call x1, Pallas kernels: 142 us -> 139 us  [call(): pl.pallas_call(functools.partial(kernel, seats), out_shape=(jax.ShapeDtyp...]
where the time goes in v5:
time: 146 us
  Pallas kernels  139 us (95%)
  local copies, waits for them, and re-layouts  5.77 us (4%)
    pallas_call x1, Pallas kernels, call(): pl.pallas_call(functools.partial(kernel, seats), out_shape=(jax.ShapeDtyp...  139 us
    unnamed x6, local copies, waits for them, and re-layouts  4 us

profile of v5, /device:TPU:1, one launch (start us, length us, event | category | flops | bytes accessed | tf_op | source)
XLA Modules:
  0.0 145.9 jit_solution(14061284104897637021)
XLA Ops:
  0.6 0.0 copy-start.1
  0.6 0.6 copy-done.1
  1.3 0.6 broadcast_in_dim.8.drow_ref
  1.9 138.6 %shard_map.50 = (bf16[128,4096]{1,0:T(8,128)(2,1)}, bf16[128,4096]{1,0:T(8,128)(2,1)}, f32[8,128]{1,0:T(8,128)}) custom-call(s32[8,128]{1,0:T(8,128)} %broadcast_in_dim.8.drow_ref, bf16[128,4096]{1,0:T(8,128)(2,1)} %q_ref.1, bf16[128,4096]{1,0:T(8,128)(2,1)} %p_ref.1), custom_call_target="tpu_custom_call" | custom-call | tf_op jit(solution)/shard_map/pallas_call | solution.py:584
  140.5 1.2 slice.3
  142.3 0.2 conditional.1
  142.6 0.0 copy-start
  142.6 2.4 %copy.11 = bf16[128,4096]{1,0:T(8,128)(2,1)} copy(bf16[128,4096]{1,0:T(8,128)(2,1)} %get-tuple-element.29) | data formatting | bytes 2097152
  145.0 0.0 copy-done
  145.0 1.0 copy.12
Async XLA Ops:
  0.6 0.7 copy-start.1
  142.6 2.4 %copy-start = (bf16[128,4096]{1,0:T(8,128)(2,1)S(1)}, bf16[128,4096]{1,0:T(8,128)(2,1)}, u32[]{:S(2)}) copy-start(bf16[128,4096]{1,0:T(8,128)(2,1)} %get-tuple-element.30) | copy-start | bytes 3145732

commit v6 on v5

--- a/solution.py
+++ b/solution.py
@@ -322,6 +322,7 @@
 
     for k in range(RAW):
         fill_own(k)
+        fill_q(k)
 
     @pl.loop(4, 7)
     def _(step):
@@ -333,8 +334,6 @@
 
     start_ring(7)
     pass_on(6)
-    fill_q(0)
-    fill_q(1)
     add_scores(5)
     for copy in plane_copies:
         copy.wait_recv()
@@ -342,9 +341,9 @@
         jnp.maximum(plane_top[...], plane_tops[0]), jnp.maximum(plane_tops[1], plane_tops[2])
     )
     pass_on(7)
-    add_scores(6)
     add_scores(0)
     add_scores(1)
+    add_scores(6)
 
     mate_seats = pl.ds((1 - c) * half_g, half_g)
 
@@ -467,23 +466,6 @@
         send_all(dp.at[k], back_p.at[k], back_s.at[1, k], back_r.at[1, k])
         back_p[k, g, 0:seats] = dp[k, g, 0:seats]
 
-    open_sums(0)
-    query_part(0)
-    open_sums(1)
-    add_sums(0)
-    query_part(1)
-
-    @pl.loop(2, CHUNKS)
-    def _(k):
-        open_sums(k)
-        add_sums(k - 1)
-        query_part(k)
-        close_sums(k - 2)
-
-    add_sums(CHUNKS - 1)
-    close_sums(CHUNKS - 2)
-    close_sums(CHUNKS - 1)
-
     def outputs(k, which):
         out, o_ref = ((out_q, oq_ref), (out_p, op_ref))[which]
         cols = pl.ds(pl.multiple_of(c * half_d + k * width, width), width)
@@ -492,17 +474,47 @@
             remote(out.at[k, 1 - c], o_ref.at[:, cols], out_s.at[which, k], out_r.at[which, k], (g, mate)),
         )
 
-    for which in range(2):
+    def finish(k, which):
         back, out = ((back_q, out_q), (back_p, out_p))[which]
-
-        @pl.loop(0, CHUNKS)
-        def _(k):
-            wait_all(back.at[k], back_r.at[which, k])
-            part = jnp.dot(unplace[...], back[k].reshape(rows, width), preferred_element_type=F32)
-            out[k] = part.astype(BF16).reshape(2, npairs, width)
-            here, there = outputs(k, which)
-            here.start()
-            there.start()
+        wait_all(back.at[k], back_r.at[which, k])
+        part = jnp.dot(unplace[...], back[k].reshape(rows, width), preferred_element_type=F32)
+        out[k] = part.astype(BF16).reshape(2, npairs, width)
+        here, there = outputs(k, which)
+        here.start()
+        there.start()
+
+    open_sums(0)
+    query_part(0)
+    open_sums(1)
+    add_sums(0)
+    query_part(1)
+
+    @pl.loop(2, 4)
+    def _(k):
+        open_sums(k)
+        add_sums(k - 1)
+        query_part(k)
+        close_sums(k - 2)
+
+    @pl.loop(4, CHUNKS)
+    def _(k):
+        open_sums(k)
+        add_sums(k - 1)
+        query_part(k)
+        close_sums(k - 2)
+        finish(k - 4, 0)
+
+    add_sums(CHUNKS - 1)
+    close_sums(CHUNKS - 2)
+    finish(4, 0)
+    finish(5, 0)
+    close_sums(CHUNKS - 1)
+    finish(6, 0)
+    finish(7, 0)
+
+    @pl.loop(0, CHUNKS)
+    def _(k):
+        finish(k, 1)
 
     @pl.loop(0, CHUNKS)
     def _(k):
@@ -545,7 +557,7 @@
     rows = n_group * SEATS
     half = rows // 2
     half_g = n_group // 2
-    drow = jnp.broadcast_to(destination.reshape(1, npairs), (8, npairs))
+    drow = destination.reshape(1, npairs)
     dma = pltpu.SemaphoreType.DMA
     in_vmem = pl.BlockSpec(memory_space=pltpu.VMEM)
     anywhere = pl.BlockSpec(memory_space=pl.ANY)
@@ -557,7 +569,7 @@
     payload = (CHUNKS, n_group, SEATS, width)
     def call(seats, collective_id):
         scratch = [
-            vm(NZ, 2, 8, npairs, dtype=jnp.int32),
+            vm(NZ, 2, 1, npairs, dtype=jnp.int32),
             vm(NZ, 2, npairs, RAW * width), vm(RAW, NZ - 1, n_group, SEATS, width),
             vm(2, npairs, half_d), vm(2, npairs, half_d),
             vm(rows, 2 * npairs), vm(2 * npairs, rows),

time: 146 us -> 144 us (0.986)
    unnamed x6 -> x4, local copies, waits for them, and re-layouts: 4 us -> 3.35 us
where the time goes in v6:
time: 144 us
  Pallas kernels  138 us (96%)
  local copies, waits for them, and re-layouts  4.55 us (3%)
    pallas_call x1, Pallas kernels, call(): pl.pallas_call(functools.partial(kernel, seats), out_shape=(jax.ShapeDtyp...  138 us
    unnamed x4, local copies, waits for them, and re-layouts  3.35 us

profile of v6, /device:TPU:1, one launch (start us, length us, event | category | flops | bytes accessed | tf_op | source)
XLA Modules:
  0.0 144.2 jit_solution(4446175325235280529)
XLA Ops:
  0.6 138.1 %shard_map.50 = (bf16[128,4096]{1,0:T(8,128)(2,1)}, bf16[128,4096]{1,0:T(8,128)(2,1)}, f32[8,128]{1,0:T(8,128)}) custom-call(s32[1,128]{1,0:T(1,128)} %bitcast.2, bf16[128,4096]{1,0:T(8,128)(2,1)} %q_ref.1, bf16[128,4096]{1,0:T(8,128)(2,1)} %p_ref.1), custom_call_target="tpu_custom_call" | custom-call | tf_op jit(solution)/shard_map/pallas_call | solution.py:596
  138.7 1.2 slice.3
  140.6 0.3 conditional.1
  140.9 0.0 copy-start
  140.9 2.4 %copy.11 = bf16[128,4096]{1,0:T(8,128)(2,1)} copy(bf16[128,4096]{1,0:T(8,128)(2,1)} %get-tuple-element.29) | data formatting | bytes 2097152
  143.3 0.0 copy-done
  143.3 1.0 copy.12
Async XLA Ops:
  140.9 2.4 %copy-start = (bf16[128,4096]{1,0:T(8,128)(2,1)S(1)}, bf16[128,4096]{1,0:T(8,128)(2,1)}, u32[]{:S(2)}) copy-start(bf16[128,4096]{1,0:T(8,128)(2,1)} %get-tuple-element.30) | copy-start | bytes 3145732
